TPU v7x, 512 devices: a whole 4x8x8 slice. The times are simulated.
512 devices in a mesh: section: 8 (over z), expert: 64 (over y, x, core).
Axes of the slice: x: 4, y: 8, z: 8, core: 2. Of those that a mesh axis runs over, the one named last changes fastest.
Arguments:
- feat_saved: bfloat16 [8, 2, 8192, 1024], P('section', None, 'expert'), may hold values from -6 to 6
- out_grad: bfloat16 [2, 8192, 1024], P(None, 'expert'), may hold values from -6 to 6
- lengths: int32 [2, 64], P(None, 'expert'), may hold values from 32 to 128, as said below
- expert_ids: int32 [8, 2, 8192], P('section', None, 'expert'), may hold values from 0 to 63, as said below
- slot_ids: int32 [8, 2, 8192], P('section', None, 'expert'), may hold values from 0 to 2, as said below
- expert_preact: bfloat16 [8, 2, 12288, 640], P('section', None, 'expert'), may hold values from -6 to 6
- conv_weight: bfloat16 [8, 32, 1024], P('section'), may hold values from -0.5 to 0.5
- norm_gain: bfloat16 [8, 1024], P('section'), may hold values from 0.5 to 1.5
- centroids: bfloat16 [8, 64, 1024], P('section'), may hold values from -0.375 to 0.375
- w_in: bfloat16 [8, 64, 1024, 640], P('section', 'expert'), may hold values from -0.1875 to 0.1875
- w_out: bfloat16 [8, 64, 640, 1024], P('section', 'expert'), may hold values from -0.25 to 0.25
Outputs:
- section_grads: bfloat16 [8, 2, 8192, 1024], P('section', None, 'expert')
Inputs may be any that keep to these rules, and one draw needn't show every extreme that they name: `expert_ids`: in every block and micro-batch, the 128 frames of one utterance name each expert at most 3 times, and one expert is named exactly 3 times by the frames of every utterance. `slot_ids`: within one utterance's frames of one block and micro-batch, the frames that name the same expert hold the slots 0, 1, ... up to their count less one, each once. `lengths`: in every micro-batch at least one utterance has all 128 frames.
All inputs are finite; a program needn't handle non-finite values.
Results may differ from a plain program's by a relative error of at most 0.02.
Values may be sent and summed in bfloat16 or wider, within the bound.
No kernel may reach another device: no remote copies, remote signals or barrier semaphores. Data moves between devices by JAX's collectives and lax.ppermute only.
A program may use at most 64 MiB of HBM per device.

v0:
```python
import math

import jax
import jax.numpy as jnp
from jax import lax
from jax.sharding import PartitionSpec as P


def shifted(block, axis, distance):
    devices = range(lax.axis_size(axis))
    route = [(i - distance, i) for i in devices if i - distance in devices]
    return lax.ppermute(block, axis, route)


def time_conv(values, kernel, low_pad):
    tap_count = kernel.shape[0]
    frames = values.shape[-2]
    widths = [(0, 0)] * (values.ndim - 2) + [(low_pad, tap_count - 1 - low_pad), (0, 0)]
    padded = jnp.pad(values, widths)
    summed = jnp.zeros_like(values)
    for tap_idx in range(tap_count):
        summed = summed + kernel[tap_idx] * lax.slice_in_dim(
            padded, tap_idx, tap_idx + frames, axis=values.ndim - 2
        )
    return summed


def gelu_parts(preact):
    act_val = preact.astype(jnp.float32)
    cdf_val = 0.5 * (1.0 + jax.scipy.special.erf(act_val * (1.0 / math.sqrt(2.0))))
    gelu_val = act_val * cdf_val
    gelu_slope = cdf_val + act_val * jnp.exp(-0.5 * act_val * act_val) * (
        1.0 / math.sqrt(2.0 * math.pi)
    )
    return (gelu_val, gelu_slope)


def contract_last(left, right):
    return lax.dot_general(
        left, right, (((1,), (1,)), ((), ())), preferred_element_type=jnp.float32
    )


def expert_whole(bucket, preact, weight_in, weight_out):
    received = lax.all_to_all(bucket, "expert", split_axis=0, concat_axis=0, tiled=True)
    recv_shape = received.shape
    slot_rows = received.reshape(recv_shape[0] * recv_shape[1], recv_shape[2])
    hidden_grad = contract_last(slot_rows, weight_out)
    gelu_val, gelu_slope = gelu_parts(preact)
    gate_grad = jnp.sum(hidden_grad * gelu_val, axis=1)
    pre_grad = (hidden_grad * gelu_slope).astype(jnp.bfloat16)
    slot_grad = contract_last(pre_grad, weight_in).astype(jnp.bfloat16)
    back_rows, back_gate = (
        lax.all_to_all(
            slot_grad.reshape(recv_shape), "expert", split_axis=0, concat_axis=0, tiled=True
        ),
        lax.all_to_all(
            gate_grad.reshape(recv_shape[0], recv_shape[1]).astype(jnp.bfloat16),
            "expert",
            split_axis=0,
            concat_axis=0,
            tiled=True,
        ).astype(jnp.float32),
    )
    return (back_rows.reshape(slot_rows.shape), back_gate.reshape(slot_rows.shape[0]))


def block_grad(
    grad_in,
    feats_b,
    length,
    routed,
    slot_pos,
    preact,
    conv_k,
    gain_vec,
    cent_table,
    weight_in,
    weight_out,
):
    frames, feat_width = feats_b.shape
    experts = cent_table.shape[0]
    slot_cap = preact.shape[0] // experts
    tap_count = conv_k.shape[0]
    feats = feats_b.astype(jnp.float32)
    frame_mask = (lax.iota(jnp.int32, frames) < length).astype(jnp.float32)[:, None]
    pre_act = time_conv(feats * frame_mask, conv_k, tap_count // 2)
    sig_pre = jax.nn.sigmoid(pre_act)
    residual = feats + frame_mask * pre_act * sig_pre
    inv_rms = lax.rsqrt(jnp.mean(residual * residual, axis=1, keepdims=True) + 1e-06)
    normed = (residual * inv_rms * gain_vec).astype(jnp.bfloat16)
    onehot_exp = (routed[:, None] == lax.iota(jnp.int32, experts)[None, :]).astype(jnp.bfloat16)
    score_all = jnp.dot(normed, cent_table.T, preferred_element_type=jnp.float32)
    score_val = jnp.sum(score_all * onehot_exp.astype(jnp.float32), axis=1)
    gate_val = jax.nn.sigmoid(score_val)
    cent_rows = jnp.dot(onehot_exp, cent_table, preferred_element_type=jnp.float32)
    grad_f = grad_in.astype(jnp.float32)
    conv_slope = frame_mask * sig_pre * (1.0 + pre_act * (1.0 - sig_pre))
    kernel_rev = conv_k[::-1]
    back_pad = tap_count - 1 - tap_count // 2
    target = routed * slot_cap + slot_pos
    onehot_slot = (lax.iota(jnp.int32, experts * slot_cap)[:, None] == target[None, :]).astype(
        jnp.bfloat16
    )
    bucket = jnp.dot(onehot_slot, grad_in, preferred_element_type=jnp.float32).astype(jnp.bfloat16)
    bucket = bucket.reshape(experts, slot_cap, feat_width)
    slot_back, gate_back = expert_whole(bucket, preact, weight_in, weight_out)
    slot_grad = lax.dot_general(
        onehot_slot, slot_back, (((0,), (0,)), ((), ())), preferred_element_type=jnp.float32
    )
    gate_grad = jnp.dot(gate_back, onehot_slot.astype(jnp.float32), precision=lax.Precision.HIGHEST)
    total_grad = (
        gate_val[:, None] * slot_grad
        + (gate_val * (1.0 - gate_val) * gate_grad)[:, None] * cent_rows
    )
    scaled = total_grad * gain_vec
    cubed = inv_rms * inv_rms * inv_rms
    norm_grad = inv_rms * scaled - residual * cubed * jnp.mean(
        residual * scaled, axis=1, keepdims=True
    )
    resid_grad = grad_f + norm_grad
    result = resid_grad + frame_mask * time_conv(conv_slope * resid_grad, kernel_rev, back_pad)
    return result.astype(jnp.bfloat16)


def on_device(
    feat_saved,
    out_grad,
    lengths,
    expert_ids,
    slot_ids,
    expert_preact,
    conv_weight,
    norm_gain,
    centroids,
    w_in,
    w_out,
):
    section_count = lax.axis_size("section")
    section_idx = lax.axis_index("section")
    micro_count = out_grad.shape[0]
    conv_k = conv_weight[0].astype(jnp.float32)
    gain_vec = norm_gain[0].astype(jnp.float32)
    cent_table = centroids[0]
    weight_in = w_in[0, 0]
    weight_out = w_out[0, 0]

    def one_tick(tick_idx, carry):
        incoming, grads = carry
        micro_pos = tick_idx - (section_count - 1 - section_idx)
        is_valid = jnp.logical_and(micro_pos >= 0, micro_pos < micro_count)
        micro_sel = jnp.clip(micro_pos, 0, micro_count - 1)

        def select_micro(array):
            return lax.dynamic_index_in_dim(array, micro_sel, 0, keepdims=False)

        grad_in = jnp.where(section_idx == section_count - 1, select_micro(out_grad), incoming)
        new_grad = block_grad(
            grad_in,
            select_micro(feat_saved[0]),
            select_micro(lengths)[0],
            select_micro(expert_ids[0]),
            select_micro(slot_ids[0]),
            select_micro(expert_preact[0]),
            conv_k,
            gain_vec,
            cent_table,
            weight_in,
            weight_out,
        )
        updated = lax.dynamic_update_index_in_dim(grads, new_grad, micro_sel, 0)
        grads = jnp.where(is_valid, updated, grads)
        incoming = shifted(new_grad, "section", -1)
        return (incoming, grads)

    start = (jnp.zeros(out_grad.shape[1:], jnp.bfloat16), jnp.zeros_like(out_grad))
    final_in, grads = lax.fori_loop(0, section_count + micro_count - 1, one_tick, start)
    return grads[None]


def solution(mesh):
    in_specs = (
        P("section", None, "expert", None),
        P(None, "expert", None),
        P(None, "expert"),
        P("section", None, "expert"),
        P("section", None, "expert"),
        P("section", None, "expert", None),
        P("section", None, None),
        P("section", None),
        P("section", None, None),
        P("section", "expert", None, None),
        P("section", "expert", None, None),
    )
    out_specs = P("section", None, "expert", None)
    return jax.shard_map(
        on_device, mesh=mesh, in_specs=in_specs, out_specs=out_specs, check_vma=False
    )
```

profile of v0, /device:TPU:1, one launch (start us, length us, event | category | flops | bytes accessed | tf_op | source)
XLA Modules:
  0.0 762.2 jit_solution(3011441828272550267)
XLA Ops:
  2.4 759.7 %while.17 = (s32[]{:T(128)}, bf16[128,1024]{1,0:T(8,128)(2,1)S(1)}, bf16[2,128,1024]{2,1,0:T(8,128)(2,1)}, pred[]{:T(512)}, s32[]{:T(128)}, /*index=5*/bf16[2,12...) while((s32[]{:T(128)}, bf16[128,1024]{1,0:T(8,128)(2,1)S(1)}, ...), condition=%wide.region_5.6_spmd, body=%wide.region_0.5_spmd.sunk | while | flops 662857024 | bytes 33682924 | solution.py:177
  5.4 11.6 %all-to-all-start = ((bf16[64,3,1024]{2,1,0:T(4,128)(2,1)}), bf16[64,3,1024]{2,1,0:T(4,128)(2,1)S(1)}, u32[]{:S(2)}, u32[]{:S(2)}) async-start(bf16[64,3,1024]{2,1,0:T(4,128)(2,1)} %reshape.162), calls=%async_computation | async-start | bytes 1048576 | tf_op jit(solution)/shard_map/while/body/eval_jaxpr/all_to_all | solution.py:45
  22.6 12.2 %all-to-all-done = bf16[64,3,1024]{2,1,0:T(4,128)(2,1)S(1)} async-done(((bf16[64,3,1024]{2,1,0:T(4,128)(2,1)}), bf16[64,3,1024]{2,1,0:T(4,128)(2,1)S(1)}, u32[]{:S(2)}, u32[]{:S(2)}) %all-to-all-start) | async-done | bytes 393248 | tf_op jit(solution)/shard_map/while/body/eval_jaxpr/all_to_all | solution.py:45
  38.6 5.7 all-to-all-start.1
  47.5 6.3 all-to-all-done.1
  59.5 16.8 %all-to-all-done.2 = bf16[64,3,1024]{2,1,0:T(4,128)(2,1)S(1)} async-done(((bf16[64,3,1024]{2,1,0:T(4,128)(2,1)}), bf16[64,3,1024]{2,1,0:T(4,128)(2,1)S(1)}, u32[]{:S(2)}, u32[]{:S(2)}) %all-to-all-start.2) | async-done | bytes 393248 | tf_op jit(solution)/shard_map/while/body/eval_jaxpr/all_to_all | solution.py:54
  82.5 9.0 %collective-permute-done = bf16[128,1024]{1,0:T(8,128)(2,1)S(1)} collective-permute-done((bf16[128,1024]{1,0:T(8,128)(2,1)S(1)}, bf16[128,1024]{1,0:T(8,128)(2,1)S(1)}, u32[]{:S(2)}, u32[]{:S(2)}) %collective-permute-start) | collective-permute-done | bytes 262176 | tf_op jit(solution)/shard_map/while/body/eval_jaxpr/ppermute | solution.py:12
  94.5 5.9 all-to-all-start
  105.9 12.2 %all-to-all-done = bf16[64,3,1024]{2,1,0:T(4,128)(2,1)S(1)} async-done(((bf16[64,3,1024]{2,1,0:T(4,128)(2,1)}), bf16[64,3,1024]{2,1,0:T(4,128)(2,1)S(1)}, u32[]{:S(2)}, u32[]{:S(2)}) %all-to-all-start) | async-done | bytes 393248 | tf_op jit(solution)/shard_map/while/body/eval_jaxpr/all_to_all | solution.py:45
  130.8 6.3 all-to-all-done.1
  142.8 16.8 %all-to-all-done.2 = bf16[64,3,1024]{2,1,0:T(4,128)(2,1)S(1)} async-done(((bf16[64,3,1024]{2,1,0:T(4,128)(2,1)}), bf16[64,3,1024]{2,1,0:T(4,128)(2,1)S(1)}, u32[]{:S(2)}, u32[]{:S(2)}) %all-to-all-start.2) | async-done | bytes 393248 | tf_op jit(solution)/shard_map/while/body/eval_jaxpr/all_to_all | solution.py:54
  165.8 9.0 %collective-permute-done = bf16[128,1024]{1,0:T(8,128)(2,1)S(1)} collective-permute-done((bf16[128,1024]{1,0:T(8,128)(2,1)S(1)}, bf16[128,1024]{1,0:T(8,128)(2,1)S(1)}, u32[]{:S(2)}, u32[]{:S(2)}) %collective-permute-start) | collective-permute-done | bytes 262176 | tf_op jit(solution)/shard_map/while/body/eval_jaxpr/ppermute | solution.py:12
  177.8 5.9 all-to-all-start
  189.2 12.2 %all-to-all-done = bf16[64,3,1024]{2,1,0:T(4,128)(2,1)S(1)} async-done(((bf16[64,3,1024]{2,1,0:T(4,128)(2,1)}), bf16[64,3,1024]{2,1,0:T(4,128)(2,1)S(1)}, u32[]{:S(2)}, u32[]{:S(2)}) %all-to-all-start) | async-done | bytes 393248 | tf_op jit(solution)/shard_map/while/body/eval_jaxpr/all_to_all | solution.py:45
  214.1 6.3 all-to-all-done.1
  226.1 16.8 %all-to-all-done.2 = bf16[64,3,1024]{2,1,0:T(4,128)(2,1)S(1)} async-done(((bf16[64,3,1024]{2,1,0:T(4,128)(2,1)}), bf16[64,3,1024]{2,1,0:T(4,128)(2,1)S(1)}, u32[]{:S(2)}, u32[]{:S(2)}) %all-to-all-start.2) | async-done | bytes 393248 | tf_op jit(solution)/shard_map/while/body/eval_jaxpr/all_to_all | solution.py:54
  249.1 9.0 %collective-permute-done = bf16[128,1024]{1,0:T(8,128)(2,1)S(1)} collective-permute-done((bf16[128,1024]{1,0:T(8,128)(2,1)S(1)}, bf16[128,1024]{1,0:T(8,128)(2,1)S(1)}, u32[]{:S(2)}, u32[]{:S(2)}) %collective-permute-start) | collective-permute-done | bytes 262176 | tf_op jit(solution)/shard_map/while/body/eval_jaxpr/ppermute | solution.py:12
  261.1 5.9 all-to-all-start
  272.5 12.2 %all-to-all-done = bf16[64,3,1024]{2,1,0:T(4,128)(2,1)S(1)} async-done(((bf16[64,3,1024]{2,1,0:T(4,128)(2,1)}), bf16[64,3,1024]{2,1,0:T(4,128)(2,1)S(1)}, u32[]{:S(2)}, u32[]{:S(2)}) %all-to-all-start) | async-done | bytes 393248 | tf_op jit(solution)/shard_map/while/body/eval_jaxpr/all_to_all | solution.py:45
  297.5 6.3 all-to-all-done.1
  309.5 16.8 %all-to-all-done.2 = bf16[64,3,1024]{2,1,0:T(4,128)(2,1)S(1)} async-done(((bf16[64,3,1024]{2,1,0:T(4,128)(2,1)}), bf16[64,3,1024]{2,1,0:T(4,128)(2,1)S(1)}, u32[]{:S(2)}, u32[]{:S(2)}) %all-to-all-start.2) | async-done | bytes 393248 | tf_op jit(solution)/shard_map/while/body/eval_jaxpr/all_to_all | solution.py:54
  332.5 10.2 %collective-permute-done = bf16[128,1024]{1,0:T(8,128)(2,1)S(1)} collective-permute-done((bf16[128,1024]{1,0:T(8,128)(2,1)S(1)}, bf16[128,1024]{1,0:T(8,128)(2,1)S(1)}, u32[]{:S(2)}, u32[]{:S(2)}) %collective-permute-start) | collective-permute-done | bytes 262176 | tf_op jit(solution)/shard_map/while/body/eval_jaxpr/ppermute | solution.py:12
  345.7 5.9 all-to-all-start
  357.1 12.2 %all-to-all-done = bf16[64,3,1024]{2,1,0:T(4,128)(2,1)S(1)} async-done(((bf16[64,3,1024]{2,1,0:T(4,128)(2,1)}), bf16[64,3,1024]{2,1,0:T(4,128)(2,1)S(1)}, u32[]{:S(2)}, u32[]{:S(2)}) %all-to-all-start) | async-done | bytes 393248 | tf_op jit(solution)/shard_map/while/body/eval_jaxpr/all_to_all | solution.py:45
  382.0 6.2 all-to-all-done.1
  394.0 16.8 %all-to-all-done.2 = bf16[64,3,1024]{2,1,0:T(4,128)(2,1)S(1)} async-done(((bf16[64,3,1024]{2,1,0:T(4,128)(2,1)}), bf16[64,3,1024]{2,1,0:T(4,128)(2,1)S(1)}, u32[]{:S(2)}, u32[]{:S(2)}) %all-to-all-start.2) | async-done | bytes 393248 | tf_op jit(solution)/shard_map/while/body/eval_jaxpr/all_to_all | solution.py:54
  417.0 9.6 %collective-permute-done = bf16[128,1024]{1,0:T(8,128)(2,1)S(1)} collective-permute-done((bf16[128,1024]{1,0:T(8,128)(2,1)S(1)}, bf16[128,1024]{1,0:T(8,128)(2,1)S(1)}, u32[]{:S(2)}, u32[]{:S(2)}) %collective-permute-start) | collective-permute-done | bytes 262176 | tf_op jit(solution)/shard_map/while/body/eval_jaxpr/ppermute | solution.py:12
  429.6 5.9 all-to-all-start
  441.0 12.2 %all-to-all-done = bf16[64,3,1024]{2,1,0:T(4,128)(2,1)S(1)} async-done(((bf16[64,3,1024]{2,1,0:T(4,128)(2,1)}), bf16[64,3,1024]{2,1,0:T(4,128)(2,1)S(1)}, u32[]{:S(2)}, u32[]{:S(2)}) %all-to-all-start) | async-done | bytes 393248 | tf_op jit(solution)/shard_map/while/body/eval_jaxpr/all_to_all | solution.py:45
  465.9 6.3 all-to-all-done.1
  477.9 16.8 %all-to-all-done.2 = bf16[64,3,1024]{2,1,0:T(4,128)(2,1)S(1)} async-done(((bf16[64,3,1024]{2,1,0:T(4,128)(2,1)}), bf16[64,3,1024]{2,1,0:T(4,128)(2,1)S(1)}, u32[]{:S(2)}, u32[]{:S(2)}) %all-to-all-start.2) | async-done | bytes 393248 | tf_op jit(solution)/shard_map/while/body/eval_jaxpr/all_to_all | solution.py:54
  500.9 9.5 %collective-permute-done = bf16[128,1024]{1,0:T(8,128)(2,1)S(1)} collective-permute-done((bf16[128,1024]{1,0:T(8,128)(2,1)S(1)}, bf16[128,1024]{1,0:T(8,128)(2,1)S(1)}, u32[]{:S(2)}, u32[]{:S(2)}) %collective-permute-start) | collective-permute-done | bytes 262176 | tf_op jit(solution)/shard_map/while/body/eval_jaxpr/ppermute | solution.py:12
  513.5 5.9 all-to-all-start
  524.9 12.2 %all-to-all-done = bf16[64,3,1024]{2,1,0:T(4,128)(2,1)S(1)} async-done(((bf16[64,3,1024]{2,1,0:T(4,128)(2,1)}), bf16[64,3,1024]{2,1,0:T(4,128)(2,1)S(1)}, u32[]{:S(2)}, u32[]{:S(2)}) %all-to-all-start) | async-done | bytes 393248 | tf_op jit(solution)/shard_map/while/body/eval_jaxpr/all_to_all | solution.py:45
  549.8 6.3 all-to-all-done.1
  561.8 16.8 %all-to-all-done.2 = bf16[64,3,1024]{2,1,0:T(4,128)(2,1)S(1)} async-done(((bf16[64,3,1024]{2,1,0:T(4,128)(2,1)}), bf16[64,3,1024]{2,1,0:T(4,128)(2,1)S(1)}, u32[]{:S(2)}, u32[]{:S(2)}) %all-to-all-start.2) | async-done | bytes 393248 | tf_op jit(solution)/shard_map/while/body/eval_jaxpr/all_to_all | solution.py:54
  584.8 9.5 %collective-permute-done = bf16[128,1024]{1,0:T(8,128)(2,1)S(1)} collective-permute-done((bf16[128,1024]{1,0:T(8,128)(2,1)S(1)}, bf16[128,1024]{1,0:T(8,128)(2,1)S(1)}, u32[]{:S(2)}, u32[]{:S(2)}) %collective-permute-start) | collective-permute-done | bytes 262176 | tf_op jit(solution)/shard_map/while/body/eval_jaxpr/ppermute | solution.py:12
  597.4 5.9 all-to-all-start
  608.8 12.2 %all-to-all-done = bf16[64,3,1024]{2,1,0:T(4,128)(2,1)S(1)} async-done(((bf16[64,3,1024]{2,1,0:T(4,128)(2,1)}), bf16[64,3,1024]{2,1,0:T(4,128)(2,1)S(1)}, u32[]{:S(2)}, u32[]{:S(2)}) %all-to-all-start) | async-done | bytes 393248 | tf_op jit(solution)/shard_map/while/body/eval_jaxpr/all_to_all | solution.py:45
  633.7 6.3 all-to-all-done.1
  645.7 16.8 %all-to-all-done.2 = bf16[64,3,1024]{2,1,0:T(4,128)(2,1)S(1)} async-done(((bf16[64,3,1024]{2,1,0:T(4,128)(2,1)}), bf16[64,3,1024]{2,1,0:T(4,128)(2,1)S(1)}, u32[]{:S(2)}, u32[]{:S(2)}) %all-to-all-start.2) | async-done | bytes 393248 | tf_op jit(solution)/shard_map/while/body/eval_jaxpr/all_to_all | solution.py:54
  668.7 9.5 %collective-permute-done = bf16[128,1024]{1,0:T(8,128)(2,1)S(1)} collective-permute-done((bf16[128,1024]{1,0:T(8,128)(2,1)S(1)}, bf16[128,1024]{1,0:T(8,128)(2,1)S(1)}, u32[]{:S(2)}, u32[]{:S(2)}) %collective-permute-start) | collective-permute-done | bytes 262176 | tf_op jit(solution)/shard_map/while/body/eval_jaxpr/ppermute | solution.py:12
  681.3 5.9 all-to-all-start
  692.7 12.2 %all-to-all-done = bf16[64,3,1024]{2,1,0:T(4,128)(2,1)S(1)} async-done(((bf16[64,3,1024]{2,1,0:T(4,128)(2,1)}), bf16[64,3,1024]{2,1,0:T(4,128)(2,1)S(1)}, u32[]{:S(2)}, u32[]{:S(2)}) %all-to-all-start) | async-done | bytes 393248 | tf_op jit(solution)/shard_map/while/body/eval_jaxpr/all_to_all | solution.py:45
  708.8 5.7 all-to-all-start.1
  717.6 6.3 all-to-all-done.1
  729.6 16.8 %all-to-all-done.2 = bf16[64,3,1024]{2,1,0:T(4,128)(2,1)S(1)} async-done(((bf16[64,3,1024]{2,1,0:T(4,128)(2,1)}), bf16[64,3,1024]{2,1,0:T(4,128)(2,1)S(1)}, u32[]{:S(2)}, u32[]{:S(2)}) %all-to-all-start.2) | async-done | bytes 393248 | tf_op jit(solution)/shard_map/while/body/eval_jaxpr/all_to_all | solution.py:54
  752.6 9.5 %collective-permute-done = bf16[128,1024]{1,0:T(8,128)(2,1)S(1)} collective-permute-done((bf16[128,1024]{1,0:T(8,128)(2,1)S(1)}, bf16[128,1024]{1,0:T(8,128)(2,1)S(1)}, u32[]{:S(2)}, u32[]{:S(2)}) %collective-permute-start) | collective-permute-done | bytes 262176 | tf_op jit(solution)/shard_map/while/body/eval_jaxpr/ppermute | solution.py:12
  (380 shorter events, 287.8 us)
Async XLA Ops:
  4.1 12.9 %copy-start.5 = (s32[2,1]{0,1:T(1,128)S(1)}, s32[2,1]{0,1:T(1,128)}, u32[]{:S(2)}) copy-start(s32[2,1]{0,1:T(1,128)} %get-tuple-element.676) | copy-start | bytes 28 | tf_op jit(solution)/shard_map/while
  4.1 14.2 %copy-start = (bf16[1,2,128,1024]{3,2,1,0:T(8,128)(2,1)S(1)}, bf16[1,2,128,1024]{3,2,1,0:T(8,128)(2,1)}, u32[]{:S(2)}) copy-start(bf16[1,2,128,1024]{3,2,1,0:T(8,128)(2,1)} %get-tuple-element.675) | copy-start | bytes 1572868 | tf_op jit(solution)/shard_map/while
  5.4 29.3 %all-to-all-start = ((bf16[64,3,1024]{2,1,0:T(4,128)(2,1)}), bf16[64,3,1024]{2,1,0:T(4,128)(2,1)S(1)}, u32[]{:S(2)}, u32[]{:S(2)}) async-start(bf16[64,3,1024]{2,1,0:T(4,128)(2,1)} %reshape.162), calls=%async_computation | async-start | bytes 1048576 | tf_op jit(solution)/shard_map/while/body/eval_jaxpr/all_to_all | solution.py:45
  38.6 15.1 %all-to-all-start.1 = ((bf16[64,1,3]{2,1,0:T(2,128)(2,1)}), bf16[64,1,3]{2,1,0:T(2,128)(2,1)S(1)}, u32[]{:S(2)}, u32[]{:S(2)}) async-start(bf16[64,1,3]{2,1,0:T(2,128)(2,1)} %convert_element_type.216), calls=%async_computation.1 | async-start | bytes 65536 | tf_op jit(solution)/shard_map/while/body/eval_jaxpr/all_to_all | solution.py:57
  46.5 12.0 %copy-start.1 = (bf16[64,1024]{1,0:T(8,128)(2,1)S(1)}, bf16[64,1024]{1,0:T(8,128)(2,1)}, u32[]{:S(2)}) copy-start(bf16[64,1024]{1,0:T(8,128)(2,1)} %get-tuple-element.679) | copy-start | bytes 393220 | tf_op jit(solution)/shard_map/while
  53.7 22.5 %all-to-all-start.2 = ((bf16[64,3,1024]{2,1,0:T(4,128)(2,1)}), bf16[64,3,1024]{2,1,0:T(4,128)(2,1)S(1)}, u32[]{:S(2)}, u32[]{:S(2)}) async-start(bf16[64,3,1024]{2,1,0:T(4,128)(2,1)} %reshape.165), calls=%async_computation.2 | async-start | bytes 1048576 | tf_op jit(solution)/shard_map/while/body/eval_jaxpr/all_to_all | solution.py:54
  81.2 10.3 %collective-permute-start = (bf16[128,1024]{1,0:T(8,128)(2,1)S(1)}, bf16[128,1024]{1,0:T(8,128)(2,1)S(1)}, u32[]{:S(2)}, u32[]{:S(2)}) collective-permute-start(bf16[128,1024]{1,0:T(8,128)(2,1)S(1)} %get-tuple-element.627), channel_id=1, source_target_pairs={{64,0},{128,64},{192,128},{256,192},{320,256},{384,320},{448,384},... | collective-permute-start | bytes 786440 | tf_op jit(solution)/shard_map/while/body/eval_jaxpr/ppermute | solution.py:12
  94.5 23.6 %all-to-all-start = ((bf16[64,3,1024]{2,1,0:T(4,128)(2,1)}), bf16[64,3,1024]{2,1,0:T(4,128)(2,1)S(1)}, u32[]{:S(2)}, u32[]{:S(2)}) async-start(bf16[64,3,1024]{2,1,0:T(4,128)(2,1)} %reshape.162), calls=%async_computation | async-start | bytes 1048576 | tf_op jit(solution)/shard_map/while/body/eval_jaxpr/all_to_all | solution.py:45
  118.4 9.3 %copy-start.4 = (bf16[1,2,192,640]{3,2,1,0:T(8,128)(2,1)S(1)}, bf16[1,2,192,640]{3,2,1,0:T(8,128)(2,1)}, u32[]{:S(2)}) copy-start(bf16[1,2,192,640]{3,2,1,0:T(8,128)(2,1)} %get-tuple-element.683) | copy-start | bytes 1474564 | tf_op jit(solution)/shard_map/while
  122.0 15.1 %all-to-all-start.1 = ((bf16[64,1,3]{2,1,0:T(2,128)(2,1)}), bf16[64,1,3]{2,1,0:T(2,128)(2,1)S(1)}, u32[]{:S(2)}, u32[]{:S(2)}) async-start(bf16[64,1,3]{2,1,0:T(2,128)(2,1)} %convert_element_type.216), calls=%async_computation.1 | async-start | bytes 65536 | tf_op jit(solution)/shard_map/while/body/eval_jaxpr/all_to_all | solution.py:57
  129.8 12.0 %copy-start.1 = (bf16[64,1024]{1,0:T(8,128)(2,1)S(1)}, bf16[64,1024]{1,0:T(8,128)(2,1)}, u32[]{:S(2)}) copy-start(bf16[64,1024]{1,0:T(8,128)(2,1)} %get-tuple-element.679) | copy-start | bytes 393220 | tf_op jit(solution)/shard_map/while
  137.1 22.5 %all-to-all-start.2 = ((bf16[64,3,1024]{2,1,0:T(4,128)(2,1)}), bf16[64,3,1024]{2,1,0:T(4,128)(2,1)S(1)}, u32[]{:S(2)}, u32[]{:S(2)}) async-start(bf16[64,3,1024]{2,1,0:T(4,128)(2,1)} %reshape.165), calls=%async_computation.2 | async-start | bytes 1048576 | tf_op jit(solution)/shard_map/while/body/eval_jaxpr/all_to_all | solution.py:54
  164.5 10.3 %collective-permute-start = (bf16[128,1024]{1,0:T(8,128)(2,1)S(1)}, bf16[128,1024]{1,0:T(8,128)(2,1)S(1)}, u32[]{:S(2)}, u32[]{:S(2)}) collective-permute-start(bf16[128,1024]{1,0:T(8,128)(2,1)S(1)} %get-tuple-element.627), channel_id=1, source_target_pairs={{64,0},{128,64},{192,128},{256,192},{320,256},{384,320},{448,384},... | collective-permute-start | bytes 786440 | tf_op jit(solution)/shard_map/while/body/eval_jaxpr/ppermute | solution.py:12
  177.8 23.6 %all-to-all-start = ((bf16[64,3,1024]{2,1,0:T(4,128)(2,1)}), bf16[64,3,1024]{2,1,0:T(4,128)(2,1)S(1)}, u32[]{:S(2)}, u32[]{:S(2)}) async-start(bf16[64,3,1024]{2,1,0:T(4,128)(2,1)} %reshape.162), calls=%async_computation | async-start | bytes 1048576 | tf_op jit(solution)/shard_map/while/body/eval_jaxpr/all_to_all | solution.py:45
  205.3 15.1 %all-to-all-start.1 = ((bf16[64,1,3]{2,1,0:T(2,128)(2,1)}), bf16[64,1,3]{2,1,0:T(2,128)(2,1)S(1)}, u32[]{:S(2)}, u32[]{:S(2)}) async-start(bf16[64,1,3]{2,1,0:T(2,128)(2,1)} %convert_element_type.216), calls=%async_computation.1 | async-start | bytes 65536 | tf_op jit(solution)/shard_map/while/body/eval_jaxpr/all_to_all | solution.py:57
  213.1 12.0 %copy-start.1 = (bf16[64,1024]{1,0:T(8,128)(2,1)S(1)}, bf16[64,1024]{1,0:T(8,128)(2,1)}, u32[]{:S(2)}) copy-start(bf16[64,1024]{1,0:T(8,128)(2,1)} %get-tuple-element.679) | copy-start | bytes 393220 | tf_op jit(solution)/shard_map/while
  220.4 22.5 %all-to-all-start.2 = ((bf16[64,3,1024]{2,1,0:T(4,128)(2,1)}), bf16[64,3,1024]{2,1,0:T(4,128)(2,1)S(1)}, u32[]{:S(2)}, u32[]{:S(2)}) async-start(bf16[64,3,1024]{2,1,0:T(4,128)(2,1)} %reshape.165), calls=%async_computation.2 | async-start | bytes 1048576 | tf_op jit(solution)/shard_map/while/body/eval_jaxpr/all_to_all | solution.py:54
  247.8 10.3 %collective-permute-start = (bf16[128,1024]{1,0:T(8,128)(2,1)S(1)}, bf16[128,1024]{1,0:T(8,128)(2,1)S(1)}, u32[]{:S(2)}, u32[]{:S(2)}) collective-permute-start(bf16[128,1024]{1,0:T(8,128)(2,1)S(1)} %get-tuple-element.627), channel_id=1, source_target_pairs={{64,0},{128,64},{192,128},{256,192},{320,256},{384,320},{448,384},... | collective-permute-start | bytes 786440 | tf_op jit(solution)/shard_map/while/body/eval_jaxpr/ppermute | solution.py:12
  261.1 23.6 %all-to-all-start = ((bf16[64,3,1024]{2,1,0:T(4,128)(2,1)}), bf16[64,3,1024]{2,1,0:T(4,128)(2,1)S(1)}, u32[]{:S(2)}, u32[]{:S(2)}) async-start(bf16[64,3,1024]{2,1,0:T(4,128)(2,1)} %reshape.162), calls=%async_computation | async-start | bytes 1048576 | tf_op jit(solution)/shard_map/while/body/eval_jaxpr/all_to_all | solution.py:45
  288.6 15.1 %all-to-all-start.1 = ((bf16[64,1,3]{2,1,0:T(2,128)(2,1)}), bf16[64,1,3]{2,1,0:T(2,128)(2,1)S(1)}, u32[]{:S(2)}, u32[]{:S(2)}) async-start(bf16[64,1,3]{2,1,0:T(2,128)(2,1)} %convert_element_type.216), calls=%async_computation.1 | async-start | bytes 65536 | tf_op jit(solution)/shard_map/while/body/eval_jaxpr/all_to_all | solution.py:57
  296.4 12.0 %copy-start.1 = (bf16[64,1024]{1,0:T(8,128)(2,1)S(1)}, bf16[64,1024]{1,0:T(8,128)(2,1)}, u32[]{:S(2)}) copy-start(bf16[64,1024]{1,0:T(8,128)(2,1)} %get-tuple-element.679) | copy-start | bytes 393220 | tf_op jit(solution)/shard_map/while
  303.7 22.5 %all-to-all-start.2 = ((bf16[64,3,1024]{2,1,0:T(4,128)(2,1)}), bf16[64,3,1024]{2,1,0:T(4,128)(2,1)S(1)}, u32[]{:S(2)}, u32[]{:S(2)}) async-start(bf16[64,3,1024]{2,1,0:T(4,128)(2,1)} %reshape.165), calls=%async_computation.2 | async-start | bytes 1048576 | tf_op jit(solution)/shard_map/while/body/eval_jaxpr/all_to_all | solution.py:54
  331.2 11.5 %collective-permute-start = (bf16[128,1024]{1,0:T(8,128)(2,1)S(1)}, bf16[128,1024]{1,0:T(8,128)(2,1)S(1)}, u32[]{:S(2)}, u32[]{:S(2)}) collective-permute-start(bf16[128,1024]{1,0:T(8,128)(2,1)S(1)} %get-tuple-element.627), channel_id=1, source_target_pairs={{64,0},{128,64},{192,128},{256,192},{320,256},{384,320},{448,384},... | collective-permute-start | bytes 786440 | tf_op jit(solution)/shard_map/while/body/eval_jaxpr/ppermute | solution.py:12
  345.7 23.6 %all-to-all-start = ((bf16[64,3,1024]{2,1,0:T(4,128)(2,1)}), bf16[64,3,1024]{2,1,0:T(4,128)(2,1)S(1)}, u32[]{:S(2)}, u32[]{:S(2)}) async-start(bf16[64,3,1024]{2,1,0:T(4,128)(2,1)} %reshape.162), calls=%async_computation | async-start | bytes 1048576 | tf_op jit(solution)/shard_map/while/body/eval_jaxpr/all_to_all | solution.py:45
  373.2 15.1 %all-to-all-start.1 = ((bf16[64,1,3]{2,1,0:T(2,128)(2,1)}), bf16[64,1,3]{2,1,0:T(2,128)(2,1)S(1)}, u32[]{:S(2)}, u32[]{:S(2)}) async-start(bf16[64,1,3]{2,1,0:T(2,128)(2,1)} %convert_element_type.216), calls=%async_computation.1 | async-start | bytes 65536 | tf_op jit(solution)/shard_map/while/body/eval_jaxpr/all_to_all | solution.py:57
  381.0 12.0 %copy-start.1 = (bf16[64,1024]{1,0:T(8,128)(2,1)S(1)}, bf16[64,1024]{1,0:T(8,128)(2,1)}, u32[]{:S(2)}) copy-start(bf16[64,1024]{1,0:T(8,128)(2,1)} %get-tuple-element.679) | copy-start | bytes 393220 | tf_op jit(solution)/shard_map/while
  388.3 22.5 %all-to-all-start.2 = ((bf16[64,3,1024]{2,1,0:T(4,128)(2,1)}), bf16[64,3,1024]{2,1,0:T(4,128)(2,1)S(1)}, u32[]{:S(2)}, u32[]{:S(2)}) async-start(bf16[64,3,1024]{2,1,0:T(4,128)(2,1)} %reshape.165), calls=%async_computation.2 | async-start | bytes 1048576 | tf_op jit(solution)/shard_map/while/body/eval_jaxpr/all_to_all | solution.py:54
  415.7 10.8 %collective-permute-start = (bf16[128,1024]{1,0:T(8,128)(2,1)S(1)}, bf16[128,1024]{1,0:T(8,128)(2,1)S(1)}, u32[]{:S(2)}, u32[]{:S(2)}) collective-permute-start(bf16[128,1024]{1,0:T(8,128)(2,1)S(1)} %get-tuple-element.627), channel_id=1, source_target_pairs={{64,0},{128,64},{192,128},{256,192},{320,256},{384,320},{448,384},... | collective-permute-start | bytes 786440 | tf_op jit(solution)/shard_map/while/body/eval_jaxpr/ppermute | solution.py:12
  429.6 23.6 %all-to-all-start = ((bf16[64,3,1024]{2,1,0:T(4,128)(2,1)}), bf16[64,3,1024]{2,1,0:T(4,128)(2,1)S(1)}, u32[]{:S(2)}, u32[]{:S(2)}) async-start(bf16[64,3,1024]{2,1,0:T(4,128)(2,1)} %reshape.162), calls=%async_computation | async-start | bytes 1048576 | tf_op jit(solution)/shard_map/while/body/eval_jaxpr/all_to_all | solution.py:45
  457.1 15.1 %all-to-all-start.1 = ((bf16[64,1,3]{2,1,0:T(2,128)(2,1)}), bf16[64,1,3]{2,1,0:T(2,128)(2,1)S(1)}, u32[]{:S(2)}, u32[]{:S(2)}) async-start(bf16[64,1,3]{2,1,0:T(2,128)(2,1)} %convert_element_type.216), calls=%async_computation.1 | async-start | bytes 65536 | tf_op jit(solution)/shard_map/while/body/eval_jaxpr/all_to_all | solution.py:57
  464.9 12.0 %copy-start.1 = (bf16[64,1024]{1,0:T(8,128)(2,1)S(1)}, bf16[64,1024]{1,0:T(8,128)(2,1)}, u32[]{:S(2)}) copy-start(bf16[64,1024]{1,0:T(8,128)(2,1)} %get-tuple-element.679) | copy-start | bytes 393220 | tf_op jit(solution)/shard_map/while
  472.2 22.5 %all-to-all-start.2 = ((bf16[64,3,1024]{2,1,0:T(4,128)(2,1)}), bf16[64,3,1024]{2,1,0:T(4,128)(2,1)S(1)}, u32[]{:S(2)}, u32[]{:S(2)}) async-start(bf16[64,3,1024]{2,1,0:T(4,128)(2,1)} %reshape.165), calls=%async_computation.2 | async-start | bytes 1048576 | tf_op jit(solution)/shard_map/while/body/eval_jaxpr/all_to_all | solution.py:54
  499.6 10.8 %collective-permute-start = (bf16[128,1024]{1,0:T(8,128)(2,1)S(1)}, bf16[128,1024]{1,0:T(8,128)(2,1)S(1)}, u32[]{:S(2)}, u32[]{:S(2)}) collective-permute-start(bf16[128,1024]{1,0:T(8,128)(2,1)S(1)} %get-tuple-element.627), channel_id=1, source_target_pairs={{64,0},{128,64},{192,128},{256,192},{320,256},{384,320},{448,384},... | collective-permute-start | bytes 786440 | tf_op jit(solution)/shard_map/while/body/eval_jaxpr/ppermute | solution.py:12
  513.5 23.6 %all-to-all-start = ((bf16[64,3,1024]{2,1,0:T(4,128)(2,1)}), bf16[64,3,1024]{2,1,0:T(4,128)(2,1)S(1)}, u32[]{:S(2)}, u32[]{:S(2)}) async-start(bf16[64,3,1024]{2,1,0:T(4,128)(2,1)} %reshape.162), calls=%async_computation | async-start | bytes 1048576 | tf_op jit(solution)/shard_map/while/body/eval_jaxpr/all_to_all | solution.py:45
  541.0 15.1 %all-to-all-start.1 = ((bf16[64,1,3]{2,1,0:T(2,128)(2,1)}), bf16[64,1,3]{2,1,0:T(2,128)(2,1)S(1)}, u32[]{:S(2)}, u32[]{:S(2)}) async-start(bf16[64,1,3]{2,1,0:T(2,128)(2,1)} %convert_element_type.216), calls=%async_computation.1 | async-start | bytes 65536 | tf_op jit(solution)/shard_map/while/body/eval_jaxpr/all_to_all | solution.py:57
  548.8 12.0 %copy-start.1 = (bf16[64,1024]{1,0:T(8,128)(2,1)S(1)}, bf16[64,1024]{1,0:T(8,128)(2,1)}, u32[]{:S(2)}) copy-start(bf16[64,1024]{1,0:T(8,128)(2,1)} %get-tuple-element.679) | copy-start | bytes 393220 | tf_op jit(solution)/shard_map/while
  556.1 22.5 %all-to-all-start.2 = ((bf16[64,3,1024]{2,1,0:T(4,128)(2,1)}), bf16[64,3,1024]{2,1,0:T(4,128)(2,1)S(1)}, u32[]{:S(2)}, u32[]{:S(2)}) async-start(bf16[64,3,1024]{2,1,0:T(4,128)(2,1)} %reshape.165), calls=%async_computation.2 | async-start | bytes 1048576 | tf_op jit(solution)/shard_map/while/body/eval_jaxpr/all_to_all | solution.py:54
  583.5 10.8 %collective-permute-start = (bf16[128,1024]{1,0:T(8,128)(2,1)S(1)}, bf16[128,1024]{1,0:T(8,128)(2,1)S(1)}, u32[]{:S(2)}, u32[]{:S(2)}) collective-permute-start(bf16[128,1024]{1,0:T(8,128)(2,1)S(1)} %get-tuple-element.627), channel_id=1, source_target_pairs={{64,0},{128,64},{192,128},{256,192},{320,256},{384,320},{448,384},... | collective-permute-start | bytes 786440 | tf_op jit(solution)/shard_map/while/body/eval_jaxpr/ppermute | solution.py:12
  597.4 23.6 %all-to-all-start = ((bf16[64,3,1024]{2,1,0:T(4,128)(2,1)}), bf16[64,3,1024]{2,1,0:T(4,128)(2,1)S(1)}, u32[]{:S(2)}, u32[]{:S(2)}) async-start(bf16[64,3,1024]{2,1,0:T(4,128)(2,1)} %reshape.162), calls=%async_computation | async-start | bytes 1048576 | tf_op jit(solution)/shard_map/while/body/eval_jaxpr/all_to_all | solution.py:45
  624.9 15.1 %all-to-all-start.1 = ((bf16[64,1,3]{2,1,0:T(2,128)(2,1)}), bf16[64,1,3]{2,1,0:T(2,128)(2,1)S(1)}, u32[]{:S(2)}, u32[]{:S(2)}) async-start(bf16[64,1,3]{2,1,0:T(2,128)(2,1)} %convert_element_type.216), calls=%async_computation.1 | async-start | bytes 65536 | tf_op jit(solution)/shard_map/while/body/eval_jaxpr/all_to_all | solution.py:57
  632.7 12.0 %copy-start.1 = (bf16[64,1024]{1,0:T(8,128)(2,1)S(1)}, bf16[64,1024]{1,0:T(8,128)(2,1)}, u32[]{:S(2)}) copy-start(bf16[64,1024]{1,0:T(8,128)(2,1)} %get-tuple-element.679) | copy-start | bytes 393220 | tf_op jit(solution)/shard_map/while
  640.0 22.5 %all-to-all-start.2 = ((bf16[64,3,1024]{2,1,0:T(4,128)(2,1)}), bf16[64,3,1024]{2,1,0:T(4,128)(2,1)S(1)}, u32[]{:S(2)}, u32[]{:S(2)}) async-start(bf16[64,3,1024]{2,1,0:T(4,128)(2,1)} %reshape.165), calls=%async_computation.2 | async-start | bytes 1048576 | tf_op jit(solution)/shard_map/while/body/eval_jaxpr/all_to_all | solution.py:54
  667.4 10.8 %collective-permute-start = (bf16[128,1024]{1,0:T(8,128)(2,1)S(1)}, bf16[128,1024]{1,0:T(8,128)(2,1)S(1)}, u32[]{:S(2)}, u32[]{:S(2)}) collective-permute-start(bf16[128,1024]{1,0:T(8,128)(2,1)S(1)} %get-tuple-element.627), channel_id=1, source_target_pairs={{64,0},{128,64},{192,128},{256,192},{320,256},{384,320},{448,384},... | collective-permute-start | bytes 786440 | tf_op jit(solution)/shard_map/while/body/eval_jaxpr/ppermute | solution.py:12
  681.3 23.6 %all-to-all-start = ((bf16[64,3,1024]{2,1,0:T(4,128)(2,1)}), bf16[64,3,1024]{2,1,0:T(4,128)(2,1)S(1)}, u32[]{:S(2)}, u32[]{:S(2)}) async-start(bf16[64,3,1024]{2,1,0:T(4,128)(2,1)} %reshape.162), calls=%async_computation | async-start | bytes 1048576 | tf_op jit(solution)/shard_map/while/body/eval_jaxpr/all_to_all | solution.py:45
  708.8 15.1 %all-to-all-start.1 = ((bf16[64,1,3]{2,1,0:T(2,128)(2,1)}), bf16[64,1,3]{2,1,0:T(2,128)(2,1)S(1)}, u32[]{:S(2)}, u32[]{:S(2)}) async-start(bf16[64,1,3]{2,1,0:T(2,128)(2,1)} %convert_element_type.216), calls=%async_computation.1 | async-start | bytes 65536 | tf_op jit(solution)/shard_map/while/body/eval_jaxpr/all_to_all | solution.py:57
  716.6 12.0 %copy-start.1 = (bf16[64,1024]{1,0:T(8,128)(2,1)S(1)}, bf16[64,1024]{1,0:T(8,128)(2,1)}, u32[]{:S(2)}) copy-start(bf16[64,1024]{1,0:T(8,128)(2,1)} %get-tuple-element.679) | copy-start | bytes 393220 | tf_op jit(solution)/shard_map/while
  723.9 22.5 %all-to-all-start.2 = ((bf16[64,3,1024]{2,1,0:T(4,128)(2,1)}), bf16[64,3,1024]{2,1,0:T(4,128)(2,1)S(1)}, u32[]{:S(2)}, u32[]{:S(2)}) async-start(bf16[64,3,1024]{2,1,0:T(4,128)(2,1)} %reshape.165), calls=%async_computation.2 | async-start | bytes 1048576 | tf_op jit(solution)/shard_map/while/body/eval_jaxpr/all_to_all | solution.py:54
  751.3 10.8 %collective-permute-start = (bf16[128,1024]{1,0:T(8,128)(2,1)S(1)}, bf16[128,1024]{1,0:T(8,128)(2,1)S(1)}, u32[]{:S(2)}, u32[]{:S(2)}) collective-permute-start(bf16[128,1024]{1,0:T(8,128)(2,1)S(1)} %get-tuple-element.627), channel_id=1, source_target_pairs={{64,0},{128,64},{192,128},{256,192},{320,256},{384,320},{448,384},... | collective-permute-start | bytes 786440 | tf_op jit(solution)/shard_map/while/body/eval_jaxpr/ppermute | solution.py:12
  (42 other events, 216.6 us)
where the time goes:
time: 767 us; the launch traced here: 762 us
  waiting for transfers between devices  402 us (52%)
  starting transfers between devices  164 us (21%)
  other arithmetic  84.6 us (11%)
  matrix products  56 us (7%)
  local copies, waits for them, and re-layouts  53.2 us (7%)
    all_to_all x9, waiting for transfers between devices, expert_whole(): lax.all_to_all(slot_grad.reshape(recv_shape), 'expert', split_axis=0, con...  151 us
    all_to_all x9, waiting for transfers between devices, expert_whole(): lax.all_to_all(bucket, 'expert', split_axis=0, concat_axis=0, tiled=True)  110 us
    ppermute x9, waiting for transfers between devices, shifted(): return lax.ppermute(block, axis, route)  84.9 us
    all_to_all x9, starting transfers between devices, expert_whole(): lax.all_to_all(bucket, 'expert', split_axis=0, concat_axis=0, tiled=True)  58.9 us
    all_to_all x9, waiting for transfers between devices, expert_whole(): lax.all_to_all(gate_grad.reshape(recv_shape[0], recv_shape[1]).astype(jnp...  56.3 us
    all_to_all x9, starting transfers between devices, expert_whole(): lax.all_to_all(gate_grad.reshape(recv_shape[0], recv_shape[1]).astype(jnp...  51.2 us
    dot_general x18, matrix products, contract_last(): lax.dot_general(left, right, (((1,), (1,)), ((), ())), preferred_element_...  44 us
    all_to_all x9, starting transfers between devices, expert_whole(): lax.all_to_all(slot_grad.reshape(recv_shape), 'expert', split_axis=0, con...  42.6 us
  transfers between devices with their start and end apart: 36, of which 36 were waited for; matrix products, arithmetic and copies ran while one was open for 11% of the time, Pallas kernels for 0%

commit v1 on v0

v1 whole, which is shorter than its diff:
```python
import functools
import math

import jax
import jax.numpy as jnp
from jax import lax
from jax.experimental import pallas as pl
from jax.experimental.pallas import tpu as pltpu
from jax.sharding import PartitionSpec as P

SUB = 8
LANES = 128
BLOCK = 8
F32 = jnp.float32
BF16 = jnp.bfloat16


def gelu_parts(preact):
    act_val = preact.astype(F32)
    cdf_val = 0.5 * (1.0 + lax.erf(act_val * (1.0 / math.sqrt(2.0))))
    gelu_val = act_val * cdf_val
    gelu_slope = cdf_val + act_val * jnp.exp(-0.5 * act_val * act_val) * (
        1.0 / math.sqrt(2.0 * math.pi)
    )
    return gelu_val, gelu_slope


def tiles(array):
    return array.reshape(array.shape[:-1] + (SUB, array.shape[-1] // SUB))


def conv_block(src_ref, taps_ref, base, reverse):
    count = taps_ref.shape[0]
    acc = [None] * BLOCK
    for j in range(BLOCK + count - 1):
        at = j + 1 if reverse else j
        row = src_ref[base + at]
        for i in range(BLOCK):
            k = i + count - at if reverse else at - i
            if 0 <= k < count:
                term = taps_ref[k] * row
                acc[i] = term if acc[i] is None else acc[i] + term
    return acc


def tile_sum(array):
    return jnp.sum(jnp.sum(array, axis=1, keepdims=True), axis=2, keepdims=True)


def prep_kernel(
    cap,
    len_ref,
    ids_ref,
    row_ref,
    info_row_ref,
    feat_ref,
    grad_ref,
    taps_ref,
    gain_ref,
    cent_ref,
    normed_ref,
    slope_ref,
    pay_ref,
    padded,
    info,
):
    micros, frames = ids_ref.shape
    half = taps_ref.shape[0] // 2
    experts = cent_ref.shape[0]
    per_expert = pay_ref.shape[0] // experts
    info_tiles = per_expert - micros * cap
    channels = feat_ref.shape[2] * feat_ref.shape[3]
    gain = gain_ref[...][None]
    pay_ref[...] = jnp.zeros_like(pay_ref)
    info[...] = jnp.zeros_like(info)
    edge = jnp.zeros((half,) + padded.shape[1:], F32)
    padded[pl.ds(0, half)] = edge
    padded[pl.ds(half + frames, half)] = edge
    lane = lax.broadcasted_iota(jnp.int32, (1, LANES), 1)

    for m in range(micros):
        length = len_ref[m]

        def fill(block, _):
            base = block * BLOCK
            time = base + lax.broadcasted_iota(jnp.int32, (BLOCK, SUB, LANES), 0)
            rows = feat_ref[m, pl.ds(base, BLOCK)].astype(F32)
            padded[pl.ds(half + base, BLOCK)] = jnp.where(time < length, rows, 0.0)
            return 0

        lax.fori_loop(0, frames // BLOCK, fill, 0)

        def step(block, _):
            base = block * BLOCK
            time = base + lax.broadcasted_iota(jnp.int32, (BLOCK, SUB, LANES), 0)
            mask = (time < length).astype(F32)
            pre = jnp.stack(conv_block(padded, taps_ref, base, False))
            sig = 1.0 / (1.0 + jnp.exp(-pre))
            residual = feat_ref[m, pl.ds(base, BLOCK)].astype(F32) + mask * pre * sig
            inv = lax.rsqrt(tile_sum(residual * residual) * (1.0 / channels) + 1e-6)
            scaled = residual * inv
            normed_ref[m, pl.ds(base, BLOCK)] = scaled.astype(BF16)
            slope_ref[m, pl.ds(base, BLOCK)] = (
                mask * sig * (1.0 + pre * (1.0 - sig))
            ).astype(BF16)
            normed = (scaled * gain).astype(BF16).astype(F32)
            cents = jnp.stack(
                [cent_ref[ids_ref[m, base + i]].astype(F32) for i in range(BLOCK)]
            )
            gate = 1.0 / (1.0 + jnp.exp(-tile_sum(normed * cents)))
            first = inv * gate
            second = first * (1.0 - gate)
            first_hi = first.astype(BF16).astype(F32)
            second_hi = second.astype(BF16).astype(F32)
            for i in range(BLOCK):
                line = jnp.where(lane == 0, first_hi[i], 0.0)
                line = jnp.where(lane == 1, first[i] - first_hi[i], line)
                line = jnp.where(lane == 2, second_hi[i], line)
                line = jnp.where(lane == 3, second[i] - second_hi[i], line)
                info[pl.ds(info_row_ref[m, base + i], 1), :] = line
                pay_ref[row_ref[m, base + i]] = grad_ref[m, base + i]
            return 0

        lax.fori_loop(0, frames // BLOCK, step, 0)

    def put_info(expert, _):
        for t in range(info_tiles):
            rows = info[pl.ds(pl.multiple_of((expert * info_tiles + t) * SUB, SUB), SUB), :]
            pay_ref[expert * per_expert + micros * cap + t] = rows.astype(BF16)
        return 0

    lax.fori_loop(0, experts, put_info, 0)


def prep(lengths, ids, slots, feats, grads, taps, gain, cents, cap):
    micros, frames = ids.shape
    experts = cents.shape[0]
    info_tiles = -(-micros * cap // SUB)
    per_expert = micros * cap + info_tiles
    which = lax.iota(jnp.int32, micros)[:, None] * cap + slots
    smem = pl.BlockSpec(memory_space=pltpu.SMEM)
    vmem = pl.BlockSpec(memory_space=pltpu.VMEM)
    normed, slope, payload = pl.pallas_call(
        functools.partial(prep_kernel, cap),
        out_shape=(
            jax.ShapeDtypeStruct(feats.shape, BF16),
            jax.ShapeDtypeStruct(feats.shape, BF16),
            jax.ShapeDtypeStruct((experts * per_expert, SUB, LANES), BF16),
        ),
        in_specs=[smem] * 4 + [vmem] * 5,
        out_specs=[vmem] * 3,
        scratch_shapes=[
            pltpu.VMEM((frames + taps.shape[0], SUB, LANES), F32),
            pltpu.VMEM((experts * info_tiles * SUB, LANES), F32),
        ],
        name="prep",
    )(
        lengths,
        ids,
        ids * per_expert + which,
        ids * (info_tiles * SUB) + which,
        feats,
        grads,
        taps,
        gain,
        cents,
    )
    return normed, slope, payload.reshape(experts, per_expert * SUB, LANES)


def expert_kernel(
    rows_ref,
    gate_ref,
    gelu_ref,
    slope_ref,
    w_out_ref,
    w_in_ref,
    cent_ref,
    gain_ref,
    out_ref,
    wide,
    left,
    total,
    gates,
):
    chunk = pl.program_id(1)
    slots = left.shape[0]

    @pl.when(chunk == 0)
    def _():
        wide[...] = rows_ref[...].reshape(wide.shape).astype(F32)
        for q in range(SUB):
            left[:, q * LANES : (q + 1) * LANES] = wide[pl.ds(q, slots, stride=SUB), :].astype(BF16)

    dims = (((1,), (1,)), ((), ()))
    gate = gate_ref[0].astype(F32)
    first = gate[:, 0:1] + gate[:, 1:2]
    hidden = lax.dot_general(left[...], w_out_ref[...], dims, preferred_element_type=F32)
    pre_grad = (hidden * slope_ref[0].astype(F32) * first).astype(BF16)
    part = lax.dot_general(pre_grad, w_in_ref[...], dims, preferred_element_type=F32)
    gated = hidden * gelu_ref[0].astype(F32)

    @pl.when(chunk == 0)
    def _():
        total[...] = part
        gates[...] = gated

    @pl.when(chunk > 0)
    def _():
        total[...] += part
        gates[...] += gated

    @pl.when(chunk == pl.num_programs(1) - 1)
    def _():
        second = gate[:, 2:3] + gate[:, 3:4]
        weight = second * jnp.sum(gates[...], axis=1, keepdims=True)
        for q in range(SUB):
            cols = slice(q * LANES, (q + 1) * LANES)
            wide[pl.ds(q, slots, stride=SUB), :] = (
                total[:, cols] + weight * cent_ref[:, cols]
            ) * gain_ref[:, cols]
        out_ref[...] = wide[...].astype(BF16).reshape(out_ref.shape)


def expert(rows, gate, gelu, slope, w_out, w_in, cent, gain):
    micros, slots, hidden = gelu.shape
    devices = rows.shape[0]
    cap = slots // devices
    width = w_in.shape[0]
    chunk = LANES
    block = (devices, cap, SUB, LANES)
    whole = pl.BlockSpec((1, width), lambda m, c: (0, 0))
    return pl.pallas_call(
        expert_kernel,
        grid=(micros, hidden // chunk),
        out_shape=jax.ShapeDtypeStruct((devices, micros * cap, SUB, LANES), BF16),
        in_specs=[
            pl.BlockSpec(block, lambda m, c: (0, m, 0, 0)),
            pl.BlockSpec((1, slots, LANES), lambda m, c: (m, 0, 0)),
            pl.BlockSpec((1, slots, chunk), lambda m, c: (m, 0, c)),
            pl.BlockSpec((1, slots, chunk), lambda m, c: (m, 0, c)),
            pl.BlockSpec((chunk, width), lambda m, c: (c, 0)),
            pl.BlockSpec((width, chunk), lambda m, c: (0, c)),
            whole,
            whole,
        ],
        out_specs=pl.BlockSpec(block, lambda m, c: (0, m, 0, 0)),
        scratch_shapes=[
            pltpu.VMEM((slots * SUB, LANES), F32),
            pltpu.VMEM((slots, width), BF16),
            pltpu.VMEM((slots, width), F32),
            pltpu.VMEM((slots, chunk), F32),
        ],
        name="expert",
    )(rows, gate, gelu, slope, w_out, w_in, cent, gain)


def frame_kernel(
    len_ref, row_ref, back_ref, grad_ref, normed_ref, slope_ref, taps_ref, out_ref, held, padded
):
    m = pl.program_id(0)
    frames = grad_ref.shape[1]
    half = taps_ref.shape[0] // 2
    channels = grad_ref.shape[2] * grad_ref.shape[3]
    length = len_ref[m]
    edge = jnp.zeros((half,) + padded.shape[1:], F32)
    padded[pl.ds(0, half)] = edge
    padded[pl.ds(half + frames, half)] = edge

    def norm(block, _):
        base = block * BLOCK
        back = jnp.stack([back_ref[row_ref[m, base + i]].astype(F32) for i in range(BLOCK)])
        normed = normed_ref[0, pl.ds(base, BLOCK)].astype(F32)
        mean = tile_sum(normed * back) * (1.0 / channels)
        resid = grad_ref[0, pl.ds(base, BLOCK)].astype(F32) + back - normed * mean
        held[pl.ds(base, BLOCK)] = resid
        padded[pl.ds(half + base, BLOCK)] = resid * slope_ref[0, pl.ds(base, BLOCK)].astype(F32)
        return 0

    lax.fori_loop(0, frames // BLOCK, norm, 0)

    def conv(block, _):
        base = block * BLOCK
        time = base + lax.broadcasted_iota(jnp.int32, (BLOCK, SUB, LANES), 0)
        summed = jnp.stack(conv_block(padded, taps_ref, base, True))
        resid = held[pl.ds(base, BLOCK)]
        out_ref[0, pl.ds(base, BLOCK)] = jnp.where(time < length, resid + summed, resid).astype(
            BF16
        )
        return 0

    lax.fori_loop(0, frames // BLOCK, conv, 0)


def frame(lengths, rows, back, grads, normed, slope, taps):
    micros, frames = rows.shape
    smem = pl.BlockSpec(memory_space=pltpu.SMEM)
    block = pl.BlockSpec((1,) + grads.shape[1:], lambda m: (m, 0, 0, 0))
    whole = lambda array: pl.BlockSpec(array.shape, lambda m: (0, 0, 0))
    return pl.pallas_call(
        frame_kernel,
        grid=(micros,),
        out_shape=jax.ShapeDtypeStruct(grads.shape, BF16),
        in_specs=[smem, smem, whole(back), block, block, block, whole(taps)],
        out_specs=block,
        scratch_shapes=[
            pltpu.VMEM((frames, SUB, LANES), F32),
            pltpu.VMEM((frames + taps.shape[0], SUB, LANES), F32),
        ],
        name="frame",
    )(lengths, rows, back, grads, normed, slope, taps)


def bucket_kernel(take_ref, row_ref, kept_ref, came_ref, bucket_ref, grad_ref):
    frames = kept_ref.shape[0]
    bucket_ref[...] = jnp.zeros_like(bucket_ref)

    def move(source):
        def step(block, _):
            base = block * BLOCK
            for i in range(BLOCK):
                row = source[base + i]
                grad_ref[base + i] = row
                bucket_ref[row_ref[base + i]] = row
            return 0

        lax.fori_loop(0, frames // BLOCK, step, 0)

    @pl.when(take_ref[0] != 0)
    def _():
        move(came_ref)

    @pl.when(take_ref[0] == 0)
    def _():
        move(kept_ref)


def bucket(take, rows, kept, came, slots):
    smem = pl.BlockSpec(memory_space=pltpu.SMEM)
    vmem = pl.BlockSpec(memory_space=pltpu.VMEM)
    return pl.pallas_call(
        bucket_kernel,
        out_shape=(
            jax.ShapeDtypeStruct((slots, SUB, LANES), BF16),
            jax.ShapeDtypeStruct(kept.shape, BF16),
        ),
        in_specs=[smem, smem, vmem, vmem],
        out_specs=[vmem, vmem],
        name="bucket",
    )(take, rows, kept, came)


def exchange(array):
    return lax.all_to_all(array, "expert", split_axis=0, concat_axis=0, tiled=True)


def on_device(
    feat_saved,
    out_grad,
    lengths,
    expert_ids,
    slot_ids,
    expert_preact,
    conv_weight,
    norm_gain,
    centroids,
    w_in,
    w_out,
):
    sections = lax.axis_size("section")
    section = lax.axis_index("section")
    experts = centroids.shape[1]
    width = centroids.shape[2]
    micros, frames = expert_ids.shape[1:]
    slots, hidden = expert_preact.shape[2:]
    cap = slots // experts
    is_odd = section % 2 == 1

    ids, slot_pos = expert_ids[0], slot_ids[0]
    taps_b = tiles(conv_weight[0])
    taps = taps_b.astype(F32)
    gain_row = norm_gain.astype(F32)
    grads = tiles(out_grad)
    normed, slope, payload = prep(
        lengths[:, 0], ids, slot_pos, tiles(feat_saved[0]), grads, taps,
        tiles(norm_gain[0]).astype(F32), tiles(centroids[0]), cap,
    )
    gelu, gelu_slope = (part.astype(BF16) for part in gelu_parts(expert_preact[0]))
    cent_b = lax.dynamic_slice_in_dim(centroids[0], lax.axis_index("expert"), 1, 0)
    cent_row = cent_b.astype(F32)

    def upward(array):
        return lax.ppermute(array, "section", [(i, i + 1) for i in range(sections - 1)])

    def mine(pair):
        return jnp.where(is_odd, pair[1], pair[0])

    def other(pair):
        return jnp.where(is_odd, pair[0], pair[1])

    target = ids * cap + slot_pos
    up_w_out = upward(w_out[0, 0])
    up_w_in = upward(w_in[0, 0])
    up_gelu = upward(other(gelu))
    up_gelu_slope = upward(other(gelu_slope))
    up_normed = upward(other(normed))
    up_slope = upward(other(slope))
    packed = jnp.concatenate(
        [
            taps_b.reshape(-1, LANES),
            cent_b.reshape(SUB, LANES),
            norm_gain.reshape(SUB, LANES),
            other(target).astype(BF16).reshape(-1, LANES),
        ]
    )
    up_packed = upward(packed)

    sent = exchange(payload).reshape(experts, -1, SUB, LANES)
    lines = sent[:, micros * cap :].reshape(experts, -1, LANES)
    gate = jnp.stack(
        [lines[:, m * cap : (m + 1) * cap].reshape(slots, LANES) for m in range(micros)]
    )
    up_gate = upward(other(gate))
    back = expert(sent, gate, gelu, gelu_slope, w_out[0, 0], w_in[0, 0], cent_row, gain_row)
    back = exchange(back.reshape(experts, -1, LANES)).reshape(-1, SUB, LANES)
    first_rows = ids * (micros * cap) + lax.iota(jnp.int32, micros)[:, None] * cap + slot_pos
    first = frame(lengths[:, 0], first_rows, back, grads, normed, slope, taps)

    size = taps_b.shape[0] * SUB
    up_taps = up_packed[:size].reshape(taps_b.shape).astype(F32)
    up_cent = up_packed[size : size + SUB].reshape(1, width).astype(F32)
    up_gain = up_packed[size + SUB : size + 2 * SUB].reshape(1, width).astype(F32)
    up_target = up_packed[size + 2 * SUB :].reshape(-1).astype(jnp.int32)
    own = (
        mine(gate), mine(gelu), mine(gelu_slope), w_out[0, 0], w_in[0, 0], cent_row, gain_row,
        mine(target), mine(normed), mine(slope), taps,
    )
    came = (
        up_gate, up_gelu, up_gelu_slope, up_w_out, up_w_in, up_cent, up_gain,
        up_target, up_normed, up_slope, up_taps,
    )
    odd_step = tuple(jnp.where(is_odd, b, a) for a, b in zip(own, came))
    even_step = tuple(jnp.where(is_odd, a, b) for a, b in zip(own, came))
    length = mine(lengths)

    kept = first[1]
    arrived = lax.ppermute(first[0], "section", [(sections - 1, sections - 2)])
    own_out, low_out = first[1], first[0]
    for k in range(1, sections):
        (gate_k, gelu_k, gelu_slope_k, w_out_k, w_in_k, cent_k, gain_k,
         target_k, normed_k, slope_k, taps_k) = odd_step if k % 2 else even_step
        take = (section == sections - 1 - k).astype(jnp.int32)
        sent, grad = bucket(take[None], target_k, kept, arrived, slots)
        sent = exchange(sent.reshape(experts, -1, LANES)).reshape(experts, cap, SUB, LANES)
        back = expert(
            sent, gate_k[None], gelu_k[None], gelu_slope_k[None], w_out_k, w_in_k, cent_k, gain_k
        )
        back = exchange(back.reshape(experts, -1, LANES)).reshape(slots, SUB, LANES)
        kept = frame(
            length, target_k[None], back, grad[None], normed_k[None], slope_k[None], taps_k
        )[0]
        if k < sections - 1:
            arrived = lax.ppermute(kept, "section", [(sections - k, sections - 2 - k)])
        own_out = jnp.where(section == sections - 1 - k, kept, own_out)
        low_out = jnp.where(section == sections - k, kept, low_out)
    top = section == sections - 1
    fetched = lax.ppermute(low_out, "section", [(i, i - 1) for i in range(1, sections)])
    rest = jnp.where(top, first[0], fetched)
    pair = jnp.stack([jnp.where(is_odd, rest, own_out), jnp.where(is_odd, own_out, rest)])
    return pair.reshape(1, micros, frames, width)


def solution(mesh):
    in_specs = (
        P("section", None, "expert", None),
        P(None, "expert", None),
        P(None, "expert"),
        P("section", None, "expert"),
        P("section", None, "expert"),
        P("section", None, "expert", None),
        P("section", None, None),
        P("section", None),
        P("section", None, None),
        P("section", "expert", None, None),
        P("section", "expert", None, None),
    )
    out_specs = P("section", None, "expert", None)
    return jax.shard_map(
        on_device, mesh=mesh, in_specs=in_specs, out_specs=out_specs, check_vma=False
    )
```

time: 767 us -> 611 us (0.80)
  waiting for transfers between devices: 402 us -> 120 us
  blocking collectives: 0 us -> 228 us
  Pallas kernels: 0 us -> 133 us
  starting transfers between devices: 164 us -> 82.3 us
  other arithmetic: 84.6 us -> 27.9 us
  matrix products: 56 us -> 0 us
  local copies, waits for them, and re-layouts: 53.2 us -> 15 us
    all_to_all x27 -> x5, waiting for transfers between devices: 317 us -> 48.2 us  [exchange(): lax.all_to_all(array, 'expert', split_axis=0, concat_axis=0, tiled=True)]
    all_to_all x0 -> x11, blocking collectives: none -> 228 us  [exchange(): lax.all_to_all(array, 'expert', split_axis=0, concat_axis=0, tiled=True)]
    pallas_call x0 -> x24, Pallas kernels: none -> 133 us  [the longest x8 60.3 us: expert(): pl.pallas_call(expert_kernel, grid=(micros, hidden // chunk), out_shape=j...]
    all_to_all x27 -> x5, starting transfers between devices: 153 us -> 42.1 us  [exchange(): lax.all_to_all(array, 'expert', split_axis=0, concat_axis=0, tiled=True)]
    dot_general x63 -> x0, matrix products: 56 us -> none  [the longest x18 44 us: contract_last(): lax.dot_general(left, right, (((1,), (1,)), ((), ())), preferred_element_...]
    reduce_sum x9 -> x0, other arithmetic: 36 us -> none  [block_grad(): jnp.mean(residual * residual, axis=1, keepdims=True) + 1e-06]
    ppermute x9 -> x16, starting transfers between devices: 11.5 us -> 40.2 us  [the longest x8 33.4 us: upward(): lax.ppermute(array, 'section', [(i, i + 1) for i in range(sections - 1)])]
    reshape x45 -> x1, local copies, waits for them, and re-layouts: 25.7 us -> 0.01 us  [on_device(): lines = sent[:, micros * cap:].reshape(experts, -1, LANES)]
  transfers between devices with their start and end apart: 36 -> 21, of which waited for: 36 -> 8; matrix products, arithmetic and copies ran while one was open for 11% -> 4% of each run, Pallas kernels for 0% -> 3%
where the time goes in v1:
time: 611 us; the launch traced here: 608 us
  blocking collectives  228 us (37%)
  Pallas kernels  133 us (22%)
  waiting for transfers between devices  120 us (20%)
  starting transfers between devices  82.3 us (13%)
  other arithmetic  27.9 us (5%)
  local copies, waits for them, and re-layouts  15 us (2%)
    all_to_all x11, blocking collectives, exchange(): lax.all_to_all(array, 'expert', split_axis=0, concat_axis=0, tiled=True)  228 us
    pallas_call x8, Pallas kernels, expert(): pl.pallas_call(expert_kernel, grid=(micros, hidden // chunk), out_shape=j...  60.3 us
    all_to_all x5, waiting for transfers between devices, exchange(): lax.all_to_all(array, 'expert', split_axis=0, concat_axis=0, tiled=True)  48.2 us
    pallas_call x8, Pallas kernels, frame(): pl.pallas_call(frame_kernel, grid=(micros,), out_shape=jax.ShapeDtypeStru...  44.2 us
    all_to_all x5, starting transfers between devices, exchange(): lax.all_to_all(array, 'expert', split_axis=0, concat_axis=0, tiled=True)  42.1 us
    ppermute x8, starting transfers between devices, upward(): lax.ppermute(array, 'section', [(i, i + 1) for i in range(sections - 1)])  33.4 us
    ppermute x6, waiting for transfers between devices, on_device(): arrived = lax.ppermute(kept, 'section', [(sections - k, sections - 2 - k)])  32.4 us
    ppermute x8, waiting for transfers between devices, upward(): lax.ppermute(array, 'section', [(i, i + 1) for i in range(sections - 1)])  30.8 us
  transfers between devices with their start and end apart: 21, of which 8 were waited for; matrix products, arithmetic and copies ran while one was open for 4% of the time, Pallas kernels for 3%

profile of v1, /device:TPU:1, one launch (start us, length us, event | category | flops | bytes accessed | tf_op | source)
XLA Modules:
  0.0 608.2 jit_solution(5599936932216038243)
XLA Ops:
  7.8 13.7 %prep.1 = (bf16[2,128,8,128]{3,2,1,0:T(8,128)(2,1)}, bf16[2,128,8,128]{3,2,1,0:T(8,128)(2,1)}, bf16[448,8,128]{2,1,0:T(8,128)(2,1)}) custom-call(s32[2]{0:T(128)} %bitcast.289, s32[2,128]{1,0:T(2,128)} %bitcast.291, s32[2,128]{1,0:T(2,128)} %get-tuple-element.76.row_ref, s32[2,128]{1,0:T(2,128)} %get-tuple-element.75.info_row_ref, ...), custom_call_target="tpu_custom_call" | custom-call | tf_op jit(solution)/shard_map/prep/pallas_call | solution.py:143
  21.5 11.7 %all-to-all-start = ((bf16[64,56,128]{2,1,0:T(8,128)(2,1)}), bf16[64,56,128]{2,1,0:T(8,128)(2,1)S(1)}, u32[]{:S(2)}, u32[]{:S(2)}) async-start(bf16[64,56,128]{2,1,0:T(8,128)(2,1)} %bitcast.258), calls=%async_computation | async-start | bytes 1835008 | tf_op jit(solution)/shard_map/all_to_all | solution.py:354
  33.4 4.0 collective-permute-start
  39.4 19.4 %all-to-all-done = bf16[64,56,128]{2,1,0:T(8,128)(2,1)S(1)} async-done(((bf16[64,56,128]{2,1,0:T(8,128)(2,1)}), bf16[64,56,128]{2,1,0:T(8,128)(2,1)S(1)}, u32[]{:S(2)}, u32[]{:S(2)}) %all-to-all-start) | async-done | bytes 917536 | tf_op jit(solution)/shard_map/all_to_all | solution.py:354
  60.4 12.1 %expert.8 = bf16[64,6,8,128]{3,2,1,0:T(8,128)(2,1)} custom-call(bf16[64,7,8,128]{3,2,1,0:T(8,128)(2,1)} %bitcast.220, bf16[2,192,128]{2,1,0:T(8,128)(2,1)} %pad_maximum_fusion.1.gate_ref, bf16[2,192,640]{2,1,0:T(8,128)(2,1)} %get-tuple-element.58.gelu_ref, bf16[2,192,640]{2,1,0:T(8,128)(2,1)} %get-tuple-element.57.slope_ref, bf16[640,1024]{1,0:T(8,128)(2,1)} %bitcast.215, ...), custom_call_target="tpu_custom_call" | custom-call | tf_op jit(solution)/shard_map/expert/pallas_call | solution.py:233
  72.6 6.4 %all-to-all-start.1 = ((bf16[64,48,128]{2,1,0:T(8,128)(2,1)}), bf16[64,48,128]{2,1,0:T(8,128)(2,1)}, u32[]{:S(2)}, u32[]{:S(2)}) async-start(bf16[64,48,128]{2,1,0:T(8,128)(2,1)} %bitcast.233), calls=%async_computation.1 | async-start | bytes 1572864 | tf_op jit(solution)/shard_map/all_to_all | solution.py:354
  79.0 5.2 collective-permute-start.6
  84.2 4.0 collective-permute-start.5
  92.8 5.2 collective-permute-start.3
  98.8 3.8 collective-permute-start.8
  105.2 8.5 %frame.8 = bf16[2,128,8,128]{3,2,1,0:T(8,128)(2,1)} custom-call(s32[2]{0:T(128)} %bitcast.290, s32[2,128]{1,0:T(2,128)} %get-tuple-element.77.row_ref, bf16[384,8,128]{2,1,0:T(8,128)(2,1)} %bitcast.12.back_ref, bf16[2,128,8,128]{3,2,1,0:T(8,128)(2,1)} %bitcast.218, bf16[2,128,8,128]{3,2,1,0:T(8,128)(2,1)} %get-tuple-element.23.normed_ref, ...), custom_call_target="tpu_custom_call" | custom-call | tf_op jit(solution)/shard_map/frame/pallas_call | solution.py:300
  115.5 28.7 %collective-permute-done.4 = bf16[192,640]{1,0:T(8,128)(2,1)S(1)} collective-permute-done((bf16[192,640]{1,0:T(8,128)(2,1)}, bf16[192,640]{1,0:T(8,128)(2,1)S(1)}, u32[]{:S(2)}, u32[]{:S(2)}) %collective-permute-start.4) | collective-permute-done | bytes 245792 | tf_op jit(solution)/shard_map/ppermute | solution.py:393
  149.5 4.7 collective-permute-start.7
  157.9 12.4 %all-to-all-start.2 = ((bf16[64,24,128]{2,1,0:T(8,128)(2,1)}), bf16[64,24,128]{2,1,0:T(8,128)(2,1)S(1)}, u32[]{:S(2)}, u32[]{:S(2)}) async-start(bf16[64,24,128]{2,1,0:T(8,128)(2,1)} %bitcast.262), calls=%async_computation.2 | async-start | bytes 786432 | tf_op jit(solution)/shard_map/all_to_all | solution.py:354
  170.4 3.2 broadcast_select_fusion
  173.6 3.4 collective-permute-start.2
  180.8 4.7 all-to-all-done.2
  186.3 6.9 %expert.9 = bf16[64,3,8,128]{3,2,1,0:T(8,128)(2,1)} custom-call(bf16[64,3,8,128]{3,2,1,0:T(8,128)(2,1)} %bitcast.244, bf16[1,192,128]{2,1,0:T(8,128)(2,1)} %get-tuple-element.66.gate_ref, bf16[1,192,640]{2,1,0:T(8,128)(2,1)} %get-tuple-element.54.gelu_ref, bf16[1,192,640]{2,1,0:T(8,128)(2,1)} %get-tuple-element.52.slope_ref, ...), custom_call_target="tpu_custom_call" | custom-call | tf_op jit(solution)/shard_map/expert/pallas_call | solution.py:233
  193.2 6.0 all-to-all-start.3
  205.4 9.0 %all-to-all-done.3 = bf16[64,24,128]{2,1,0:T(8,128)(2,1)S(1)} async-done(((bf16[64,24,128]{2,1,0:T(8,128)(2,1)}), bf16[64,24,128]{2,1,0:T(8,128)(2,1)S(1)}, u32[]{:S(2)}, u32[]{:S(2)}) %all-to-all-start.3) | async-done | bytes 393248 | tf_op jit(solution)/shard_map/all_to_all | solution.py:354
  215.2 5.1 frame.9
  223.9 20.7 %all_to_all.80 = bf16[64,24,128]{2,1,0:T(8,128)(2,1)} all-to-all(bf16[64,24,128]{2,1,0:T(8,128)(2,1)} %bitcast.263), channel_id=1, replica_groups=mesh['section'=8,'expert'=64] {'expert'}, dimensions={0} | all-to-all | bytes 786432 | tf_op jit(solution)/shard_map/all_to_all | solution.py:354
  244.6 6.9 %expert.10 = bf16[64,3,8,128]{3,2,1,0:T(8,128)(2,1)} custom-call(bf16[64,3,8,128]{3,2,1,0:T(8,128)(2,1)} %bitcast.247, bf16[1,192,128]{2,1,0:T(8,128)(2,1)} %get-tuple-element.65.gate_ref, bf16[1,192,640]{2,1,0:T(8,128)(2,1)} %get-tuple-element.53.gelu_ref, bf16[1,192,640]{2,1,0:T(8,128)(2,1)} %get-tuple-element.51.slope_ref, ...), custom_call_target="tpu_custom_call" | custom-call | tf_op jit(solution)/shard_map/expert/pallas_call | solution.py:233
  251.4 20.7 %all_to_all.81 = bf16[64,24,128]{2,1,0:T(8,128)(2,1)} all-to-all(bf16[64,24,128]{2,1,0:T(8,128)(2,1)} %bitcast.251), channel_id=1, replica_groups=mesh['section'=8,'expert'=64] {'expert'}, dimensions={0} | all-to-all | bytes 786432 | tf_op jit(solution)/shard_map/all_to_all | solution.py:354
  272.2 5.1 frame.10
  280.8 20.7 %all_to_all.82 = bf16[64,24,128]{2,1,0:T(8,128)(2,1)} all-to-all(bf16[64,24,128]{2,1,0:T(8,128)(2,1)} %bitcast.264), channel_id=1, replica_groups=mesh['section'=8,'expert'=64] {'expert'}, dimensions={0} | all-to-all | bytes 786432 | tf_op jit(solution)/shard_map/all_to_all | solution.py:354
  301.5 6.9 %expert.11 = bf16[64,3,8,128]{3,2,1,0:T(8,128)(2,1)} custom-call(bf16[64,3,8,128]{3,2,1,0:T(8,128)(2,1)} %bitcast.252, bf16[1,192,128]{2,1,0:T(8,128)(2,1)} %get-tuple-element.66.gate_ref, bf16[1,192,640]{2,1,0:T(8,128)(2,1)} %get-tuple-element.54.gelu_ref, bf16[1,192,640]{2,1,0:T(8,128)(2,1)} %get-tuple-element.52.slope_ref, ...), custom_call_target="tpu_custom_call" | custom-call | tf_op jit(solution)/shard_map/expert/pallas_call | solution.py:233
  308.4 20.7 %all_to_all.83 = bf16[64,24,128]{2,1,0:T(8,128)(2,1)} all-to-all(bf16[64,24,128]{2,1,0:T(8,128)(2,1)} %bitcast.253), channel_id=1, replica_groups=mesh['section'=8,'expert'=64] {'expert'}, dimensions={0} | all-to-all | bytes 786432 | tf_op jit(solution)/shard_map/all_to_all | solution.py:354
  329.1 5.1 frame.11
  337.7 20.7 %all_to_all.84 = bf16[64,24,128]{2,1,0:T(8,128)(2,1)} all-to-all(bf16[64,24,128]{2,1,0:T(8,128)(2,1)} %bitcast.265), channel_id=1, replica_groups=mesh['section'=8,'expert'=64] {'expert'}, dimensions={0} | all-to-all | bytes 786432 | tf_op jit(solution)/shard_map/all_to_all | solution.py:354
  358.5 6.9 %expert.12 = bf16[64,3,8,128]{3,2,1,0:T(8,128)(2,1)} custom-call(bf16[64,3,8,128]{3,2,1,0:T(8,128)(2,1)} %bitcast.254, bf16[1,192,128]{2,1,0:T(8,128)(2,1)} %get-tuple-element.65.gate_ref, bf16[1,192,640]{2,1,0:T(8,128)(2,1)} %get-tuple-element.53.gelu_ref, bf16[1,192,640]{2,1,0:T(8,128)(2,1)} %get-tuple-element.51.slope_ref, ...), custom_call_target="tpu_custom_call" | custom-call | tf_op jit(solution)/shard_map/expert/pallas_call | solution.py:233
  365.3 20.7 %all_to_all.85 = bf16[64,24,128]{2,1,0:T(8,128)(2,1)} all-to-all(bf16[64,24,128]{2,1,0:T(8,128)(2,1)} %bitcast.255), channel_id=1, replica_groups=mesh['section'=8,'expert'=64] {'expert'}, dimensions={0} | all-to-all | bytes 786432 | tf_op jit(solution)/shard_map/all_to_all | solution.py:354
  386.0 5.1 frame.12
  394.7 20.7 %all_to_all.86 = bf16[64,24,128]{2,1,0:T(8,128)(2,1)} all-to-all(bf16[64,24,128]{2,1,0:T(8,128)(2,1)} %bitcast.266), channel_id=1, replica_groups=mesh['section'=8,'expert'=64] {'expert'}, dimensions={0} | all-to-all | bytes 786432 | tf_op jit(solution)/shard_map/all_to_all | solution.py:354
  415.4 6.9 %expert.13 = bf16[64,3,8,128]{3,2,1,0:T(8,128)(2,1)} custom-call(bf16[64,3,8,128]{3,2,1,0:T(8,128)(2,1)} %bitcast.256, bf16[1,192,128]{2,1,0:T(8,128)(2,1)} %get-tuple-element.66.gate_ref, bf16[1,192,640]{2,1,0:T(8,128)(2,1)} %get-tuple-element.54.gelu_ref, bf16[1,192,640]{2,1,0:T(8,128)(2,1)} %get-tuple-element.52.slope_ref, ...), custom_call_target="tpu_custom_call" | custom-call | tf_op jit(solution)/shard_map/expert/pallas_call | solution.py:233
  422.3 20.7 %all_to_all.87 = bf16[64,24,128]{2,1,0:T(8,128)(2,1)} all-to-all(bf16[64,24,128]{2,1,0:T(8,128)(2,1)} %bitcast.257), channel_id=1, replica_groups=mesh['section'=8,'expert'=64] {'expert'}, dimensions={0} | all-to-all | bytes 786432 | tf_op jit(solution)/shard_map/all_to_all | solution.py:354
  443.0 5.1 frame.13
  451.9 20.7 %all_to_all.88 = bf16[64,24,128]{2,1,0:T(8,128)(2,1)} all-to-all(bf16[64,24,128]{2,1,0:T(8,128)(2,1)} %bitcast.267), channel_id=1, replica_groups=mesh['section'=8,'expert'=64] {'expert'}, dimensions={0} | all-to-all | bytes 786432 | tf_op jit(solution)/shard_map/all_to_all | solution.py:354
  472.6 6.9 %expert.14 = bf16[64,3,8,128]{3,2,1,0:T(8,128)(2,1)} custom-call(bf16[64,3,8,128]{3,2,1,0:T(8,128)(2,1)} %bitcast.248, bf16[1,192,128]{2,1,0:T(8,128)(2,1)} %get-tuple-element.65.gate_ref, bf16[1,192,640]{2,1,0:T(8,128)(2,1)} %get-tuple-element.53.gelu_ref, bf16[1,192,640]{2,1,0:T(8,128)(2,1)} %get-tuple-element.51.slope_ref, ...), custom_call_target="tpu_custom_call" | custom-call | tf_op jit(solution)/shard_map/expert/pallas_call | solution.py:233
  479.5 20.7 %all_to_all.89 = bf16[64,24,128]{2,1,0:T(8,128)(2,1)} all-to-all(bf16[64,24,128]{2,1,0:T(8,128)(2,1)} %bitcast.249), channel_id=1, replica_groups=mesh['section'=8,'expert'=64] {'expert'}, dimensions={0} | all-to-all | bytes 786432 | tf_op jit(solution)/shard_map/all_to_all | solution.py:354
  500.2 5.1 frame.14
  506.6 32.3 %collective-permute-done.14.came_ref = bf16[128,8,128]{2,1,0:T(8,128)(2,1)S(1)} collective-permute-done((bf16[128,8,128]{2,1,0:T(8,128)(2,1)}, bf16[128,8,128]{2,1,0:T(8,128)(2,1)S(1)}, u32[]{:S(2)}, u32[]{:S(2)}) %collective-permute-start.14) | collective-permute-done | bytes 262176 | tf_op jit(solution)/shard_map/ppermute | solution.py:463
  541.8 21.0 %all_to_all.90 = bf16[64,24,128]{2,1,0:T(8,128)(2,1)} all-to-all(bf16[64,24,128]{2,1,0:T(8,128)(2,1)} %bitcast.268), channel_id=1, replica_groups=mesh['section'=8,'expert'=64] {'expert'}, dimensions={0} | all-to-all | bytes 786432 | tf_op jit(solution)/shard_map/all_to_all | solution.py:354
  562.8 6.9 %expert.15 = bf16[64,3,8,128]{3,2,1,0:T(8,128)(2,1)} custom-call(bf16[64,3,8,128]{3,2,1,0:T(8,128)(2,1)} %bitcast.250, bf16[1,192,128]{2,1,0:T(8,128)(2,1)} %get-tuple-element.66.gate_ref, bf16[1,192,640]{2,1,0:T(8,128)(2,1)} %get-tuple-element.54.gelu_ref, bf16[1,192,640]{2,1,0:T(8,128)(2,1)} %get-tuple-element.52.slope_ref, ...), custom_call_target="tpu_custom_call" | custom-call | tf_op jit(solution)/shard_map/expert/pallas_call | solution.py:233
  569.8 5.5 all-to-all-start.15
  575.3 15.2 %all-to-all-done.15 = bf16[64,24,128]{2,1,0:T(8,128)(2,1)S(1)} async-done(((bf16[64,24,128]{2,1,0:T(8,128)(2,1)}), bf16[64,24,128]{2,1,0:T(8,128)(2,1)S(1)}, u32[]{:S(2)}, u32[]{:S(2)}) %all-to-all-start.15) | async-done | bytes 393248 | tf_op jit(solution)/shard_map/all_to_all | solution.py:354
  591.2 5.1 frame.15
  598.8 8.2 %collective-permute-done.15 = bf16[128,8,128]{2,1,0:T(8,128)(2,1)S(1)} collective-permute-done((bf16[128,8,128]{2,1,0:T(8,128)(2,1)S(1)}, bf16[128,8,128]{2,1,0:T(8,128)(2,1)S(1)}, u32[]{:S(2)}, u32[]{:S(2)}) %collective-permute-start.15) | collective-permute-done | bytes 262176 | tf_op jit(solution)/shard_map/ppermute | solution.py:467
  (158 shorter events, 67.0 us)
Async XLA Ops:
  0.0 6.4 %copy-start.34 = (bf16[1,64,1024]{2,1,0:T(8,128)(2,1)S(1)}, bf16[1,64,1024]{2,1,0:T(8,128)(2,1)}, u32[]{:S(2)}) copy-start(bf16[1,64,1024]{2,1,0:T(8,128)(2,1)} %param.19) | copy-start | bytes 393220
  0.9 6.2 %copy-start.40 = (s32[1,2,128]{2,1,0:T(2,128)S(1)}, s32[1,2,128]{2,1,0:T(2,128)}, u32[]{:S(2)}) copy-start(s32[1,2,128]{2,1,0:T(2,128)} %param.14) | copy-start | bytes 3076
  7.7 25.5 %copy-start.23 = (bf16[1,32,1024]{2,1,0:T(8,128)(2,1)S(1)}, bf16[1,32,1024]{2,1,0:T(8,128)(2,1)}, u32[]{:S(2)}) copy-start(bf16[1,32,1024]{2,1,0:T(8,128)(2,1)} %param.17) | copy-start | bytes 196612
  21.5 15.9 %copy-start.22 = (bf16[1,2,192,640]{3,2,1,0:T(8,128)(2,1)S(1)}, bf16[1,2,192,640]{3,2,1,0:T(8,128)(2,1)}, u32[]{:S(2)}) copy-start(bf16[1,2,192,640]{3,2,1,0:T(8,128)(2,1)} %param.16) | copy-start | bytes 1474564
  21.5 37.3 %all-to-all-start = ((bf16[64,56,128]{2,1,0:T(8,128)(2,1)}), bf16[64,56,128]{2,1,0:T(8,128)(2,1)S(1)}, u32[]{:S(2)}, u32[]{:S(2)}) async-start(bf16[64,56,128]{2,1,0:T(8,128)(2,1)} %bitcast.258), calls=%async_computation | async-start | bytes 1835008 | tf_op jit(solution)/shard_map/all_to_all | solution.py:354
  33.4 5.4 collective-permute-start
  38.8 21.6 %copy-start.35 = (bf16[273,128]{1,0:T(8,128)(2,1)}, bf16[273,128]{1,0:T(8,128)(2,1)S(1)}, u32[]{:S(2)}) copy-start(bf16[273,128]{1,0:T(8,128)(2,1)S(1)} %collective-permute-done) | copy-start | bytes 209668
  60.4 18.5 %copy-start.3 = (bf16[1,1,1024,640]{3,2,1,0:T(8,128)(2,1)S(1)}, bf16[1,1,1024,640]{3,2,1,0:T(8,128)(2,1)}, u32[]{:S(2)}) copy-start(bf16[1,1,1024,640]{3,2,1,0:T(8,128)(2,1)} %param.20) | copy-start | bytes 3932164
  72.6 15.6 %copy-start.2 = (bf16[2,192,640]{2,1,0:T(8,128)(2,1)S(1)}, bf16[2,192,640]{2,1,0:T(8,128)(2,1)}, u32[]{:S(2)}) copy-start(bf16[2,192,640]{2,1,0:T(8,128)(2,1)} %get-tuple-element.57.slope_ref) | copy-start | bytes 1474564
  72.6 19.5 %copy-start.1 = (bf16[2,192,640]{2,1,0:T(8,128)(2,1)S(1)}, bf16[2,192,640]{2,1,0:T(8,128)(2,1)}, u32[]{:S(2)}) copy-start(bf16[2,192,640]{2,1,0:T(8,128)(2,1)} %get-tuple-element.58.gelu_ref) | copy-start | bytes 1474564
  72.6 32.6 %all-to-all-start.1 = ((bf16[64,48,128]{2,1,0:T(8,128)(2,1)}), bf16[64,48,128]{2,1,0:T(8,128)(2,1)}, u32[]{:S(2)}, u32[]{:S(2)}) async-start(bf16[64,48,128]{2,1,0:T(8,128)(2,1)} %bitcast.233), calls=%async_computation.1 | async-start | bytes 1572864 | tf_op jit(solution)/shard_map/all_to_all | solution.py:354
  79.0 19.0 %copy-start.7 = (bf16[2,128,8,128]{3,2,1,0:T(8,128)(2,1)S(1)}, bf16[2,128,8,128]{3,2,1,0:T(8,128)(2,1)}, u32[]{:S(2)}) copy-start(bf16[2,128,8,128]{3,2,1,0:T(8,128)(2,1)} %get-tuple-element.24.slope_ref) | copy-start | bytes 1572868
  79.0 23.6 %copy-start.5 = (bf16[2,128,8,128]{3,2,1,0:T(8,128)(2,1)S(1)}, bf16[2,128,8,128]{3,2,1,0:T(8,128)(2,1)}, u32[]{:S(2)}) copy-start(bf16[2,128,8,128]{3,2,1,0:T(8,128)(2,1)} %get-tuple-element.23.normed_ref) | copy-start | bytes 1572868
  79.0 91.4 %collective-permute-start.6 = (bf16[1024,640]{1,0:T(8,128)(2,1)S(1)}, bf16[1024,640]{1,0:T(8,128)(2,1)}, u32[]{:S(2)}, u32[]{:S(2)}) collective-permute-start(bf16[1024,640]{1,0:T(8,128)(2,1)S(1)} %bitcast.214), channel_id=1, source_target_pairs={{0,64},{64,128},{128,192},{192,256},{256,320},{320,384},{384,448},... | collective-permute-start | bytes 3932168 | tf_op jit(solution)/shard_map/ppermute | solution.py:393
  84.2 92.8 %collective-permute-start.5 = (bf16[640,1024]{1,0:T(8,128)(2,1)}, bf16[640,1024]{1,0:T(8,128)(2,1)}, u32[]{:S(2)}, u32[]{:S(2)}) collective-permute-start(bf16[640,1024]{1,0:T(8,128)(2,1)} %bitcast.216), channel_id=1, source_target_pairs={{0,64},{64,128},{128,192},{192,256},{256,320},{320,384},{384,448},... | collective-permute-start | bytes 3932168 | tf_op jit(solution)/shard_map/ppermute | solution.py:393
  89.0 14.4 %copy-start.37 = (f32[1,1024]{1,0:T(1,128)S(1)}, f32[1,1024]{1,0:T(1,128)}, u32[]{:S(2)}) copy-start(f32[1,1024]{1,0:T(1,128)} %get-tuple-element.42.cent_ref) | copy-start | bytes 12292
  89.0 14.4 %copy-start.38 = (bf16[1,1024]{1,0:T(2,128)(2,1)S(1)}, bf16[1,1024]{1,0:T(2,128)(2,1)}, u32[]{:S(2)}) copy-start(bf16[1,1024]{1,0:T(2,128)(2,1)} %param.18) | copy-start | bytes 6148
  89.0 55.2 %collective-permute-start.4 = (bf16[192,640]{1,0:T(8,128)(2,1)}, bf16[192,640]{1,0:T(8,128)(2,1)S(1)}, u32[]{:S(2)}, u32[]{:S(2)}) collective-permute-start(bf16[192,640]{1,0:T(8,128)(2,1)} %select_bitcast_fusion.2), channel_id=1, source_target_pairs={{0,64},{64,128},{128,192},{192,256},{256,320},{320,384},{384,448},... | collective-permute-start | bytes 737288 | tf_op jit(solution)/shard_map/ppermute | solution.py:393
  92.8 56.6 %collective-permute-start.3 = (bf16[192,640]{1,0:T(8,128)(2,1)}, bf16[192,640]{1,0:T(8,128)(2,1)S(1)}, u32[]{:S(2)}, u32[]{:S(2)}) collective-permute-start(bf16[192,640]{1,0:T(8,128)(2,1)} %select_bitcast_fusion.3), channel_id=1, source_target_pairs={{0,64},{64,128},{128,192},{192,256},{256,320},{320,384},{384,448},... | collective-permute-start | bytes 737288 | tf_op jit(solution)/shard_map/ppermute | solution.py:393
  98.8 103.0 %collective-permute-start.8 = (bf16[128,8,128]{2,1,0:T(8,128)(2,1)}, bf16[128,8,128]{2,1,0:T(8,128)(2,1)}, u32[]{:S(2)}, u32[]{:S(2)}) collective-permute-start(bf16[128,8,128]{2,1,0:T(8,128)(2,1)} %select_bitcast_fusion), channel_id=1, source_target_pairs={{0,64},{64,128},{128,192},{192,256},{256,320},{320,384},{384,448},... | collective-permute-start | bytes 786440 | tf_op jit(solution)/shard_map/ppermute | solution.py:393
  144.9 10.1 %collective-permute-start.1 = (bf16[128,8,128]{2,1,0:T(8,128)(2,1)S(1)}, bf16[128,8,128]{2,1,0:T(8,128)(2,1)S(1)}, u32[]{:S(2)}, u32[]{:S(2)}) collective-permute-start(bf16[128,8,128]{2,1,0:T(8,128)(2,1)S(1)} %get-tuple-element.55), channel_id=1, source_target_pairs={{448,384},{449,385},{450,386},{451,387},{452,388},{453,389},{454,3... | collective-permute-start | bytes 786440 | tf_op jit(solution)/shard_map/ppermute | solution.py:447
  149.5 54.2 %collective-permute-start.7 = (bf16[128,8,128]{2,1,0:T(8,128)(2,1)}, bf16[128,8,128]{2,1,0:T(8,128)(2,1)}, u32[]{:S(2)}, u32[]{:S(2)}) collective-permute-start(bf16[128,8,128]{2,1,0:T(8,128)(2,1)} %select_bitcast_fusion.1), channel_id=1, source_target_pairs={{0,64},{64,128},{128,192},{192,256},{256,320},{320,384},{384,448},... | collective-permute-start | bytes 786440 | tf_op jit(solution)/shard_map/ppermute | solution.py:393
  157.9 27.6 %all-to-all-start.2 = ((bf16[64,24,128]{2,1,0:T(8,128)(2,1)}), bf16[64,24,128]{2,1,0:T(8,128)(2,1)S(1)}, u32[]{:S(2)}, u32[]{:S(2)}) async-start(bf16[64,24,128]{2,1,0:T(8,128)(2,1)} %bitcast.262), calls=%async_computation.2 | async-start | bytes 786432 | tf_op jit(solution)/shard_map/all_to_all | solution.py:354
  170.4 6.7 %copy-start.4 = (bf16[1,1,640,1024]{3,2,1,0:T(8,128)(2,1)S(1)}, bf16[1,1,640,1024]{3,2,1,0:T(8,128)(2,1)}, u32[]{:S(2)}) copy-start(bf16[1,1,640,1024]{3,2,1,0:T(8,128)(2,1)} %param.21) | copy-start | bytes 3932164
  173.6 6.5 %copy-start.31 = (bf16[64,3,128]{2,1,0:T(4,128)(2,1)S(1)}, bf16[64,3,128]{2,1,0:T(4,128)(2,1)}, u32[]{:S(2)}) copy-start(bf16[64,3,128]{2,1,0:T(4,128)(2,1)} %get-tuple-element.61) | copy-start | bytes 147460
  173.6 6.5 %collective-permute-start.2 = (bf16[192,128]{1,0:T(8,128)(2,1)S(1)}, bf16[192,128]{1,0:T(8,128)(2,1)S(1)}, u32[]{:S(2)}, u32[]{:S(2)}) collective-permute-start(bf16[192,128]{1,0:T(8,128)(2,1)S(1)} %select_n.331), channel_id=1, source_target_pairs={{0,64},{64,128},{128,192},{192,256},{256,320},{320,384},{384,448},... | collective-permute-start | bytes 147464 | tf_op jit(solution)/shard_map/ppermute | solution.py:393
  186.3 13.0 %copy-start.39 = (s32[2,1]{0,1:T(1,128)S(1)}, s32[2,1]{0,1:T(1,128)}, u32[]{:S(2)}) copy-start(s32[2,1]{0,1:T(1,128)} %param.13) | copy-start | bytes 28
  186.3 14.8 %copy-start.17 = (f32[4,8,8,128]{3,2,1,0:T(8,128)S(1)}, f32[4,8,8,128]{3,2,1,0:T(8,128)}, u32[]{:S(2)}) copy-start(f32[4,8,8,128]{3,2,1,0:T(8,128)} %copy.14) | copy-start | bytes 393220
  186.3 14.8 %copy-start.36 = (bf16[273,128]{1,0:T(8,128)(2,1)S(1)}, bf16[273,128]{1,0:T(8,128)(2,1)}, u32[]{:S(2)}) copy-start(bf16[273,128]{1,0:T(8,128)(2,1)} %copy-done.35) | copy-start | bytes 209668
  193.2 8.6 %copy-start.8 = (bf16[2,128,8,128]{3,2,1,0:T(8,128)(2,1)S(1)}, bf16[2,128,8,128]{3,2,1,0:T(8,128)(2,1)}, u32[]{:S(2)}) copy-start(bf16[2,128,8,128]{3,2,1,0:T(8,128)(2,1)} %get-tuple-element.24.slope_ref) | copy-start | bytes 1572868
  193.2 10.4 %copy-start.6 = (bf16[2,128,8,128]{3,2,1,0:T(8,128)(2,1)S(1)}, bf16[2,128,8,128]{3,2,1,0:T(8,128)(2,1)}, u32[]{:S(2)}) copy-start(bf16[2,128,8,128]{3,2,1,0:T(8,128)(2,1)} %get-tuple-element.23.normed_ref) | copy-start | bytes 1572868
  193.2 21.2 %all-to-all-start.3 = ((bf16[64,24,128]{2,1,0:T(8,128)(2,1)}), bf16[64,24,128]{2,1,0:T(8,128)(2,1)S(1)}, u32[]{:S(2)}, u32[]{:S(2)}) async-start(bf16[64,24,128]{2,1,0:T(8,128)(2,1)} %bitcast.245), calls=%async_computation.3 | async-start | bytes 786432 | tf_op jit(solution)/shard_map/all_to_all | solution.py:354
  220.3 0.7 collective-permute-start.9
  277.3 0.7 collective-permute-start.10
  334.2 0.7 collective-permute-start.11
  391.1 0.7 collective-permute-start.12
  448.1 0.9 collective-permute-start.13
  505.3 33.6 %collective-permute-start.14 = (bf16[128,8,128]{2,1,0:T(8,128)(2,1)}, bf16[128,8,128]{2,1,0:T(8,128)(2,1)S(1)}, u32[]{:S(2)}, u32[]{:S(2)}) collective-permute-start(bf16[128,8,128]{2,1,0:T(8,128)(2,1)} %bitcast.231), channel_id=1, source_target_pairs={{128,0},{129,1},{130,2},{131,3},{132,4},{133,5},{134,6},{135,7},{1... | collective-permute-start | bytes 786440 | tf_op jit(solution)/shard_map/ppermute | solution.py:463
  569.7 26.6 %copy-start = (bf16[2,128,8,128]{3,2,1,0:T(8,128)(2,1)S(1)}, bf16[2,128,8,128]{3,2,1,0:T(8,128)(2,1)}, u32[]{:S(2)}) copy-start(bf16[2,128,8,128]{3,2,1,0:T(8,128)(2,1)} %frame.8) | copy-start | bytes 1572868
  569.7 26.6 %copy-start.10 = (bf16[1,128,8,128]{3,2,1,0:T(8,128)(2,1)S(1)}, bf16[1,128,8,128]{3,2,1,0:T(8,128)(2,1)}, u32[]{:S(2)}) copy-start(bf16[1,128,8,128]{3,2,1,0:T(8,128)(2,1)} %frame.9) | copy-start | bytes 786436
  569.7 26.6 %copy-start.11 = (bf16[1,128,8,128]{3,2,1,0:T(8,128)(2,1)S(1)}, bf16[1,128,8,128]{3,2,1,0:T(8,128)(2,1)}, u32[]{:S(2)}) copy-start(bf16[1,128,8,128]{3,2,1,0:T(8,128)(2,1)} %frame.10) | copy-start | bytes 786436
  569.7 26.6 %copy-start.12 = (bf16[1,128,8,128]{3,2,1,0:T(8,128)(2,1)S(1)}, bf16[1,128,8,128]{3,2,1,0:T(8,128)(2,1)}, u32[]{:S(2)}) copy-start(bf16[1,128,8,128]{3,2,1,0:T(8,128)(2,1)} %frame.11) | copy-start | bytes 786436
  569.7 26.6 %copy-start.13 = (bf16[1,128,8,128]{3,2,1,0:T(8,128)(2,1)S(1)}, bf16[1,128,8,128]{3,2,1,0:T(8,128)(2,1)}, u32[]{:S(2)}) copy-start(bf16[1,128,8,128]{3,2,1,0:T(8,128)(2,1)} %frame.12) | copy-start | bytes 786436
  569.7 26.6 %copy-start.14 = (bf16[1,128,8,128]{3,2,1,0:T(8,128)(2,1)S(1)}, bf16[1,128,8,128]{3,2,1,0:T(8,128)(2,1)}, u32[]{:S(2)}) copy-start(bf16[1,128,8,128]{3,2,1,0:T(8,128)(2,1)} %frame.13) | copy-start | bytes 786436
  569.7 26.6 %copy-start.15 = (bf16[1,128,8,128]{3,2,1,0:T(8,128)(2,1)S(1)}, bf16[1,128,8,128]{3,2,1,0:T(8,128)(2,1)}, u32[]{:S(2)}) copy-start(bf16[1,128,8,128]{3,2,1,0:T(8,128)(2,1)} %frame.14) | copy-start | bytes 786436
  569.8 20.7 %all-to-all-start.15 = ((bf16[64,24,128]{2,1,0:T(8,128)(2,1)}), bf16[64,24,128]{2,1,0:T(8,128)(2,1)S(1)}, u32[]{:S(2)}, u32[]{:S(2)}) async-start(bf16[64,24,128]{2,1,0:T(8,128)(2,1)} %bitcast.246), calls=%async_computation.15 | async-start | bytes 786432 | tf_op jit(solution)/shard_map/all_to_all | solution.py:354
  596.3 10.6 %copy-start.16 = (bf16[1,128,8,128]{3,2,1,0:T(8,128)(2,1)S(1)}, bf16[1,128,8,128]{3,2,1,0:T(8,128)(2,1)}, u32[]{:S(2)}) copy-start(bf16[1,128,8,128]{3,2,1,0:T(8,128)(2,1)} %frame.15) | copy-start | bytes 786436
  597.5 9.5 %collective-permute-start.15 = (bf16[128,8,128]{2,1,0:T(8,128)(2,1)S(1)}, bf16[128,8,128]{2,1,0:T(8,128)(2,1)S(1)}, u32[]{:S(2)}, u32[]{:S(2)}) collective-permute-start(bf16[128,8,128]{2,1,0:T(8,128)(2,1)S(1)} %bitcast_select_fusion.1), channel_id=1, source_target_pairs={{64,0},{128,64},{192,128},{256,192},{320,256},{384,320},{448,384},... | collective-permute-start | bytes 786440 | tf_op jit(solution)/shard_map/ppermute | solution.py:467
  (15 other events, 24.4 us)

commit v2 on v1

v2 whole, which is shorter than its diff:
```python
import functools
import math

import jax
import jax.numpy as jnp
from jax import lax
from jax.experimental import pallas as pl
from jax.experimental.pallas import tpu as pltpu
from jax.sharding import PartitionSpec as P


SUB = 8
LANES = 128
BLOCK = 8
F32 = jnp.float32
BF16 = jnp.bfloat16
PARAMS = pltpu.CompilerParams(vmem_limit_bytes=16 * 2**20)
SMEM = pl.BlockSpec(memory_space=pltpu.SMEM)
VMEM = pl.BlockSpec(memory_space=pltpu.VMEM)


def gelu_parts(preact):
    act_val = preact.astype(F32)
    cdf_val = 0.5 * (1.0 + lax.erf(act_val * (1.0 / math.sqrt(2.0))))
    gelu_val = act_val * cdf_val
    gelu_slope = cdf_val + act_val * jnp.exp(-0.5 * act_val * act_val) * (
        1.0 / math.sqrt(2.0 * math.pi)
    )
    return gelu_val.astype(BF16), gelu_slope.astype(BF16)


def conv_block(src_ref, taps_ref, base, reverse):
    count = taps_ref.shape[0]
    acc = [None] * BLOCK
    for j in range(BLOCK + count - 1):
        at = j + 1 if reverse else j
        row = src_ref[base + at]
        for i in range(BLOCK):
            k = i + count - at if reverse else at - i
            if 0 <= k < count:
                term = taps_ref[k] * row
                acc[i] = term if acc[i] is None else acc[i] + term
    return jnp.stack(acc)


def tile_sum(array):
    return jnp.sum(jnp.sum(array, axis=1, keepdims=True), axis=2, keepdims=True)


def clear_edges(padded, half):
    edge = jnp.zeros((half,) + padded.shape[1:], F32)
    padded[pl.ds(0, half)] = edge
    padded[pl.ds(padded.shape[0] - half, half)] = edge


def block_time(base):
    return base + lax.broadcasted_iota(jnp.int32, (BLOCK, SUB, LANES), 0)


def to_tiles(flat_ref, rows):
    count = rows.shape[0]
    for q in range(SUB):
        flat_ref[pl.ds(q, count, stride=SUB), :] = rows[:, q * LANES : (q + 1) * LANES].astype(F32)


def prep_kernel(
    cap,
    odd_ref,
    len_ref,
    ids_ref,
    slot_ref,
    feat_ref,
    grad_ref,
    taps_ref,
    gain_ref,
    cent_ref,
    *refs,
):
    normed_refs, slope_refs, grads_refs = refs[0:2], refs[2:4], refs[4:6]
    taps_out, pay_ref, padded, flat, cents, gain_flat, info = refs[6:]
    micros, frames = ids_ref.shape
    half = taps_ref.shape[0] // 2
    experts, channels = cent_ref.shape
    per_expert = pay_ref.shape[0] // experts
    info_tiles = per_expert - micros * cap
    pay_ref[...] = jnp.zeros_like(pay_ref)
    info[...] = jnp.zeros_like(info)
    clear_edges(padded, half)
    to_tiles(flat, taps_ref[...])
    taps_out[...] = flat[pl.ds(0, taps_ref.shape[0] * SUB), :].reshape(taps_out.shape)
    to_tiles(cents, cent_ref[...])
    to_tiles(gain_flat, gain_ref[...])
    gain = gain_flat[...][None]
    lane = lax.broadcasted_iota(jnp.int32, (BLOCK, 1, LANES), 2)

    for s in range(micros):
        m = s ^ odd_ref[0]
        length = len_ref[m]
        to_tiles(flat, grad_ref[m])

        def place(block, _, s=s, m=m):
            base = block * BLOCK
            rows = flat[pl.ds(pl.multiple_of(base * SUB, BLOCK * SUB), BLOCK * SUB), :]
            rows = rows.reshape(BLOCK, SUB, LANES).astype(BF16)
            grads_refs[s][pl.ds(base, BLOCK)] = rows
            for i in range(BLOCK):
                at = ids_ref[m, base + i] * per_expert + s * cap + slot_ref[m, base + i]
                pay_ref[at] = rows[i]
            return 0

        lax.fori_loop(0, frames // BLOCK, place, 0)
        to_tiles(flat, feat_ref[m])

        def fill(block, _, length=length):
            base = block * BLOCK
            rows = flat[pl.ds(pl.multiple_of(base * SUB, BLOCK * SUB), BLOCK * SUB), :]
            rows = rows.reshape(BLOCK, SUB, LANES)
            padded[pl.ds(half + base, BLOCK)] = jnp.where(block_time(base) < length, rows, 0.0)
            return 0

        lax.fori_loop(0, frames // BLOCK, fill, 0)

        def step(block, _, s=s, m=m, length=length):
            base = block * BLOCK
            mask = (block_time(base) < length).astype(F32)
            pre = conv_block(padded, taps_out, base, False)
            sig = 1.0 / (1.0 + jnp.exp(-pre))
            rows = flat[pl.ds(pl.multiple_of(base * SUB, BLOCK * SUB), BLOCK * SUB), :]
            residual = rows.reshape(BLOCK, SUB, LANES) + mask * pre * sig
            inv = lax.rsqrt(tile_sum(residual * residual) * (1.0 / channels) + 1e-6)
            scaled = residual * inv
            normed_refs[s][pl.ds(base, BLOCK)] = scaled.astype(BF16)
            slope_refs[s][pl.ds(base, BLOCK)] = (
                mask * sig * (1.0 + pre * (1.0 - sig))
            ).astype(BF16)
            normed = (scaled * gain).astype(BF16).astype(F32)
            lines = jnp.stack(
                [
                    cents[pl.ds(pl.multiple_of(ids_ref[m, base + i] * SUB, SUB), SUB), :]
                    for i in range(BLOCK)
                ]
            )
            gate = 1.0 / (1.0 + jnp.exp(-tile_sum(normed * lines)))
            first = inv * gate
            second = first * (1.0 - gate)
            first_hi = first.astype(BF16).astype(F32)
            second_hi = second.astype(BF16).astype(F32)
            line = jnp.where(lane == 0, first_hi, 0.0)
            line = jnp.where(lane == 1, first - first_hi, line)
            line = jnp.where(lane == 2, second_hi, line)
            line = jnp.where(lane == 3, second - second_hi, line)
            for i in range(BLOCK):
                at = ids_ref[m, base + i] * (info_tiles * SUB) + s * cap + slot_ref[m, base + i]
                info[pl.ds(at, 1), :] = line[i]
            return 0

        lax.fori_loop(0, frames // BLOCK, step, 0)

    def put_info(expert, _):
        for t in range(info_tiles):
            rows = info[pl.ds(pl.multiple_of((expert * info_tiles + t) * SUB, SUB), SUB), :]
            pay_ref[expert * per_expert + micros * cap + t] = rows.astype(BF16)
        return 0

    lax.fori_loop(0, experts, put_info, 0, unroll=4)


def prep(odd, lengths, ids, slots, feats, grads, taps, gain, cents, cap):
    micros, frames = ids.shape
    experts = cents.shape[0]
    info_tiles = -(-micros * cap // SUB)
    per_expert = micros * cap + info_tiles
    count = taps.shape[0]
    one = jax.ShapeDtypeStruct((frames, SUB, LANES), BF16)
    outs = pl.pallas_call(
        functools.partial(prep_kernel, cap),
        out_shape=(one,) * 6
        + (
            jax.ShapeDtypeStruct((count, SUB, LANES), F32),
            jax.ShapeDtypeStruct((experts * per_expert, SUB, LANES), BF16),
        ),
        in_specs=[SMEM] * 4 + [VMEM] * 5,
        out_specs=[VMEM] * 8,
        scratch_shapes=[
            pltpu.VMEM((frames + count, SUB, LANES), F32),
            pltpu.VMEM((max(frames, count) * SUB, LANES), F32),
            pltpu.VMEM((experts * SUB, LANES), F32),
            pltpu.VMEM((SUB, LANES), F32),
            pltpu.VMEM((experts * info_tiles * SUB, LANES), F32),
        ],
        name="prep",
    )(odd, lengths, ids, slots, feats, grads, taps, gain, cents)
    payload = outs[7].reshape(experts, per_expert * SUB, LANES)
    return outs[0:2], outs[2:4], outs[4:6], outs[6], payload


def expert_rows(rows, gate, gelu_ref, slope_ref, w_out_ref, w_in_ref, cent_ref, gain_ref, wide, left):
    slots = left.shape[0]
    wide[...] = rows.reshape(wide.shape).astype(F32)
    for q in range(SUB):
        left[:, q * LANES : (q + 1) * LANES] = wide[pl.ds(q, slots, stride=SUB), :].astype(BF16)
    dims = (((1,), (1,)), ((), ()))
    first = gate[:, 0:1] + gate[:, 1:2]
    second = gate[:, 2:3] + gate[:, 3:4]
    hidden = lax.dot_general(left[...], w_out_ref[...], dims, preferred_element_type=F32)
    pre_grad = (hidden * slope_ref[...].astype(F32) * first).astype(BF16)
    total = lax.dot_general(pre_grad, w_in_ref[...], dims, preferred_element_type=F32)
    weight = second * jnp.sum(hidden * gelu_ref[...].astype(F32), axis=1, keepdims=True)
    for q in range(SUB):
        cols = slice(q * LANES, (q + 1) * LANES)
        wide[pl.ds(q, slots, stride=SUB), :] = (
            total[:, cols] + weight * cent_ref[:, cols]
        ) * gain_ref[:, cols]
    return wide[...].astype(BF16)


def expert_kernel(rows_ref, gate_ref, *refs):
    out_ref, wide, left = refs[6:]
    gate = gate_ref[...].astype(F32)
    out_ref[...] = expert_rows(rows_ref[...], gate, *refs[:6], wide, left).reshape(out_ref.shape)


def expert(rows, gate, *operands):
    slots = gate.shape[0]
    width = operands[3].shape[0]
    return pl.pallas_call(
        expert_kernel,
        out_shape=jax.ShapeDtypeStruct(rows.shape, BF16),
        in_specs=[VMEM] * 8,
        out_specs=VMEM,
        scratch_shapes=[pltpu.VMEM((slots * SUB, LANES), F32), pltpu.VMEM((slots, width), BF16)],
        compiler_params=PARAMS,
        name="expert",
    )(rows, gate, *operands)


def first_expert_kernel(rows_ref, *refs):
    gelu_refs, slope_refs, shared = refs[0:2], refs[2:4], refs[4:8]
    out_ref, gate_refs, wide, left, info, gate = refs[8], refs[9:11], *refs[11:]
    devices, tiles = rows_ref.shape[:2]
    cap = left.shape[0] // devices
    micros = len(gelu_refs)
    per_device = (tiles - micros * cap) * SUB
    info[...] = rows_ref[:, micros * cap :].reshape(info.shape).astype(F32)
    for s in range(micros):
        for j in range(cap):
            gate[pl.ds(j, devices, stride=cap), :] = info[
                pl.ds(s * cap + j, devices, stride=per_device), :
            ]
        gate_refs[s][...] = gate[...].astype(BF16)
        back = expert_rows(
            rows_ref[:, s * cap : (s + 1) * cap],
            gate[...], gelu_refs[s], slope_refs[s], *shared, wide, left,
        )
        out_ref[:, s * cap : (s + 1) * cap] = back.reshape(devices, cap, SUB, LANES)


def first_expert(rows, gelus, slopes, *shared):
    slots = gelus[0].shape[0]
    devices, tiles = rows.shape[:2]
    width = shared[1].shape[0]
    micros = len(gelus)
    shown = micros * slots // devices
    line = jax.ShapeDtypeStruct((slots, LANES), BF16)
    return pl.pallas_call(
        first_expert_kernel,
        out_shape=(jax.ShapeDtypeStruct((devices, shown, SUB, LANES), BF16), line, line),
        in_specs=[VMEM] * 9,
        out_specs=[VMEM] * 3,
        scratch_shapes=[
            pltpu.VMEM((slots * SUB, LANES), F32),
            pltpu.VMEM((slots, width), BF16),
            pltpu.VMEM((devices * (tiles - shown) * SUB, LANES), F32),
            pltpu.VMEM((slots, LANES), F32),
        ],
        compiler_params=PARAMS,
        name="first_expert",
    )(rows, *gelus, *slopes, *shared)


def frame_kernel(
    take_ref, len_ref, row_ref, back_ref, kept_ref, came_ref, normed_ref, slope_ref, taps_ref,
    out_ref, held, padded,
):
    frames = kept_ref.shape[0]
    half = taps_ref.shape[0] // 2
    channels = kept_ref.shape[1] * kept_ref.shape[2]
    length = len_ref[0]
    take = take_ref[0] != 0
    clear_edges(padded, half)

    def norm(block, _):
        base = block * BLOCK
        rows = pl.ds(base, BLOCK)
        back = jnp.stack([back_ref[row_ref[base + i]].astype(F32) for i in range(BLOCK)])
        normed = normed_ref[rows].astype(F32)
        mean = tile_sum(normed * back) * (1.0 / channels)
        grad = jnp.where(take, came_ref[rows].astype(F32), kept_ref[rows].astype(F32))
        resid = grad + back - normed * mean
        held[rows] = resid
        padded[pl.ds(half + base, BLOCK)] = resid * slope_ref[rows].astype(F32)
        return 0

    lax.fori_loop(0, frames // BLOCK, norm, 0, unroll=4)

    def conv(block, _):
        base = block * BLOCK
        summed = conv_block(padded, taps_ref, base, True)
        resid = held[pl.ds(base, BLOCK)]
        out = jnp.where(block_time(base) < length, resid + summed, resid)
        out_ref[pl.ds(base, BLOCK)] = out.astype(BF16)
        return 0

    lax.fori_loop(0, frames // BLOCK, conv, 0)


def frame(take, length, rows, back, kept, came, normed, slope, taps):
    frames = kept.shape[0]
    return pl.pallas_call(
        frame_kernel,
        out_shape=jax.ShapeDtypeStruct(kept.shape, BF16),
        in_specs=[SMEM] * 3 + [VMEM] * 6,
        out_specs=VMEM,
        scratch_shapes=[
            pltpu.VMEM((frames, SUB, LANES), F32),
            pltpu.VMEM((frames + taps.shape[0], SUB, LANES), F32),
        ],
        compiler_params=PARAMS,
        name="frame",
    )(take, length, rows, back, kept, came, normed, slope, taps)


def bucket_kernel(take_ref, row_ref, kept_ref, came_ref, bucket_ref):
    frames = kept_ref.shape[0]
    bucket_ref[...] = jnp.zeros_like(bucket_ref)

    def move(source):
        def step(block, _):
            base = block * BLOCK
            for i in range(BLOCK):
                bucket_ref[row_ref[base + i]] = source[base + i]
            return 0

        lax.fori_loop(0, frames // BLOCK, step, 0)

    @pl.when(take_ref[0] != 0)
    def _():
        move(came_ref)

    @pl.when(take_ref[0] == 0)
    def _():
        move(kept_ref)


def bucket(take, rows, kept, came, slots):
    return pl.pallas_call(
        bucket_kernel,
        out_shape=jax.ShapeDtypeStruct((slots, SUB, LANES), BF16),
        in_specs=[SMEM, SMEM, VMEM, VMEM],
        out_specs=VMEM,
        compiler_params=PARAMS,
        name="bucket",
    )(take, rows, kept, came)


def exchange(array):
    return lax.all_to_all(array, "expert", split_axis=0, concat_axis=0, tiled=True)


def on_device(
    feat_saved,
    out_grad,
    lengths,
    expert_ids,
    slot_ids,
    expert_preact,
    conv_weight,
    norm_gain,
    centroids,
    w_in,
    w_out,
):
    sections = lax.axis_size("section")
    section = lax.axis_index("section")
    experts, width = centroids.shape[1:]
    micros, frames = expert_ids.shape[1:]
    slots = expert_preact.shape[2]
    cap = slots // experts
    odd = section % 2
    is_odd = odd == 1

    def upward(array):
        return lax.ppermute(array, "section", [(i, i + 1) for i in range(sections - 1)])

    def pick(array, which):
        return lax.dynamic_index_in_dim(array, which, 0, keepdims=False)

    own_w_out, own_w_in = w_out[0, 0], w_in[0, 0]
    up_w_out = upward(own_w_out)
    up_w_in = upward(own_w_in)
    gain_row = norm_gain.astype(F32)
    cent_b = lax.dynamic_slice_in_dim(centroids[0], lax.axis_index("expert"), 1, 0)
    cent_row = cent_b.astype(F32)
    normed, slope, grads, taps, payload = prep(
        odd[None], lengths[:, 0], expert_ids[0], slot_ids[0], feat_saved[0], out_grad,
        conv_weight[0], norm_gain, centroids[0], cap,
    )
    gelu, gelu_slope = zip(
        *(gelu_parts(pick(expert_preact[0], which)) for which in (odd, 1 - odd))
    )

    ids = [pick(expert_ids[0], which) for which in (odd, 1 - odd)]
    slot_pos = [pick(slot_ids[0], which) for which in (odd, 1 - odd)]
    target = [i * cap + s for i, s in zip(ids, slot_pos)]
    packed = jnp.concatenate(
        [
            taps.astype(BF16).reshape(-1, LANES),
            cent_b.reshape(SUB, LANES),
            norm_gain.reshape(SUB, LANES),
            target[1].astype(BF16).reshape(-1, LANES),
        ]
    )
    up_gelu = upward(gelu[1])
    up_gelu_slope = upward(gelu_slope[1])
    up_packed = upward(packed)
    up_normed = upward(normed[1])
    up_slope = upward(slope[1])

    sent = exchange(payload).reshape(experts, -1, SUB, LANES)
    back, gate, other_gate = first_expert(
        sent, gelu, gelu_slope, own_w_out, own_w_in, cent_row, gain_row
    )
    up_gate = upward(other_gate)
    back = exchange(back.reshape(experts, -1, LANES)).reshape(-1, SUB, LANES)
    none = jnp.zeros((1,), jnp.int32)
    own_length = pick(lengths, odd)
    first = [None, None]
    for s in (1, 0):
        rows = ids[s] * (micros * cap) + s * cap + slot_pos[s]
        first[s] = frame(
            none, pick(lengths, 1 - odd) if s else own_length, rows, back,
            grads[s], grads[s], normed[s], slope[s], taps,
        )
        if s:
            arrived = lax.ppermute(first[s], "section", [(sections - 1, sections - 2)])
    kept = first[0]

    size = taps.shape[0] * SUB
    came = (
        up_gate,
        up_gelu,
        up_gelu_slope,
        up_w_out,
        up_w_in,
        up_packed[size : size + SUB].reshape(1, width).astype(F32),
        up_packed[size + SUB : size + 2 * SUB].reshape(1, width).astype(F32),
        up_packed[size + 2 * SUB :].reshape(-1).astype(jnp.int32),
        up_normed,
        up_slope,
        up_packed[:size].reshape(taps.shape).astype(F32),
    )
    own = (
        gate, gelu[0], gelu_slope[0], own_w_out, own_w_in, cent_row, gain_row,
        target[0], normed[0], slope[0], taps,
    )
    own = lax.optimization_barrier(own)
    steps = {1: tuple(jnp.where(is_odd, b, a) for a, b in zip(own, came))}

    own_out = low_out = kept
    for k in range(1, sections):
        if k == 2:
            own, came, kept = lax.optimization_barrier((own, came, kept))
            steps[0] = tuple(jnp.where(is_odd, a, b) for a, b in zip(own, came))
        operands = steps[k % 2]
        rows = operands[7]
        take = (section == sections - 1 - k).astype(jnp.int32)[None]
        sent = bucket(take, rows, kept, arrived, slots)
        sent = exchange(sent.reshape(experts, -1, LANES)).reshape(experts, cap, SUB, LANES)
        back = expert(sent, *operands[:7])
        back = exchange(back.reshape(experts, -1, LANES)).reshape(slots, SUB, LANES)
        kept = frame(take, own_length, rows, back, kept, arrived, *operands[8:])
        if k < sections - 1:
            arrived = lax.ppermute(kept, "section", [(sections - k, sections - 2 - k)])
        own_out = jnp.where(section == sections - 1 - k, kept, own_out)
        low_out = jnp.where(section == sections - k, kept, low_out)
    fetched = lax.ppermute(low_out, "section", [(i, i - 1) for i in range(1, sections)])
    rest = jnp.where(section == sections - 1, first[1], fetched)
    pair = jnp.stack([jnp.where(is_odd, rest, own_out), jnp.where(is_odd, own_out, rest)])
    return pair.reshape(1, micros, frames, width)


def solution(mesh):
    in_specs = (
        P("section", None, "expert", None),
        P(None, "expert", None),
        P(None, "expert"),
        P("section", None, "expert"),
        P("section", None, "expert"),
        P("section", None, "expert", None),
        P("section", None, None),
        P("section", None),
        P("section", None, None),
        P("section", "expert", None, None),
        P("section", "expert", None, None),
    )
    out_specs = P("section", None, "expert", None)

    return jax.shard_map(
        on_device, mesh=mesh, in_specs=in_specs, out_specs=out_specs, check_vma=False
    )
```

time: 611 us -> 545 us (0.89)
  Pallas kernels: 133 us -> 75.1 us
  blocking collectives: 228 us -> 184 us
  starting transfers between devices: 82.3 us -> 97.1 us
  local copies, waits for them, and re-layouts: 15 us -> 28.7 us
    pallas_call x24 -> x25, Pallas kernels: 133 us -> 75.1 us  [the longest x9 35.7 us: frame(): pl.pallas_call(frame_kernel, out_shape=jax.ShapeDtypeStruct(kept.shape, B...]
    all_to_all x11 -> x9, blocking collectives: 228 us -> 184 us  [exchange(): lax.all_to_all(array, 'expert', split_axis=0, concat_axis=0, tiled=True)]
    all_to_all x5 -> x7, waiting for transfers between devices: 48.2 us -> 75.7 us  [exchange(): lax.all_to_all(array, 'expert', split_axis=0, concat_axis=0, tiled=True)]
    ppermute x8, waiting for transfers between devices: 30.8 us -> 13.1 us  [upward(): lax.ppermute(array, 'section', [(i, i + 1) for i in range(sections - 1)])]
    unnamed x88 -> x190, local copies, waits for them, and re-layouts: 12.2 us -> 27.8 us
    all_to_all x5 -> x7, starting transfers between devices: 42.1 us -> 53.7 us  [exchange(): lax.all_to_all(array, 'expert', split_axis=0, concat_axis=0, tiled=True)]
    select_n x11 -> x19, other arithmetic: 13.2 us -> 21.7 us  [the longest x8 14 us: on_device(): steps[0] = tuple((jnp.where(is_odd, a, b) for a, b in zip(own, came)))]
    broadcast_in_dim x5 -> x0, other arithmetic: 6.92 us -> none  [the longest x1 1.81 us: on_device(): slope_k[None]]
  transfers between devices with their start and end apart: 21 -> 23, of which waited for: 8 -> 9; matrix products, arithmetic and copies ran while one was open for 4% -> 5% of each run, Pallas kernels for 3% -> 3%
where the time goes in v2:
time: 545 us; the launch traced here: 541 us
  blocking collectives  184 us (34%)
  waiting for transfers between devices  126 us (23%)
  starting transfers between devices  97.1 us (18%)
  Pallas kernels  75.1 us (14%)
  other arithmetic  29.6 us (5%)
  local copies, waits for them, and re-layouts  28.7 us (5%)
    all_to_all x9, blocking collectives, exchange(): lax.all_to_all(array, 'expert', split_axis=0, concat_axis=0, tiled=True)  184 us
    all_to_all x7, waiting for transfers between devices, exchange(): lax.all_to_all(array, 'expert', split_axis=0, concat_axis=0, tiled=True)  75.7 us
    all_to_all x7, starting transfers between devices, exchange(): lax.all_to_all(array, 'expert', split_axis=0, concat_axis=0, tiled=True)  53.7 us
    pallas_call x9, Pallas kernels, frame(): pl.pallas_call(frame_kernel, out_shape=jax.ShapeDtypeStruct(kept.shape, B...  35.7 us
    ppermute x8, starting transfers between devices, upward(): lax.ppermute(array, 'section', [(i, i + 1) for i in range(sections - 1)])  34 us
    ppermute x6, waiting for transfers between devices, on_device(): arrived = lax.ppermute(kept, 'section', [(sections - k, sections - 2 - k)])  29.3 us
    unnamed x190, local copies, waits for them, and re-layouts  27.8 us
    pallas_call x1, Pallas kernels, prep(): pl.pallas_call(functools.partial(prep_kernel, cap), out_shape=(one,) * 6...  15.1 us
  transfers between devices with their start and end apart: 23, of which 9 were waited for; matrix products, arithmetic and copies ran while one was open for 5% of the time, Pallas kernels for 3%

profile of v2, /device:TPU:1, one launch (start us, length us, event | category | flops | bytes accessed | tf_op | source)
XLA Modules:
  0.0 541.3 jit_solution(11576444850845697378)
XLA Ops:
  0.0 15.1 %prep.1 = (bf16[128,8,128]{2,1,0:T(8,128)(2,1)}, bf16[128,8,128]{2,1,0:T(8,128)(2,1)}, bf16[128,8,128]{2,1,0:T(8,128)(2,1)}, bf16[128,8,128]{2,1,0:T(8,128)(2,1)...) custom-call(s32[1]{0:T(128)} %bitcast.2.odd_ref, ...), custom_call_target="tpu_custom_call" | custom-call | tf_op jit(solution)/shard_map/prep/pallas_call | solution.py:175
  15.1 11.6 %all-to-all-start = ((bf16[64,56,128]{2,1,0:T(8,128)(2,1)}), bf16[64,56,128]{2,1,0:T(8,128)(2,1)S(1)}, u32[]{:S(2)}, u32[]{:S(2)}) async-start(bf16[64,56,128]{2,1,0:T(8,128)(2,1)} %bitcast.124), calls=%async_computation | async-start | bytes 1835008 | tf_op jit(solution)/shard_map/all_to_all | solution.py:367
  26.7 5.1 collective-permute-start.5
  35.4 16.8 %all-to-all-done = bf16[64,56,128]{2,1,0:T(8,128)(2,1)S(1)} async-done(((bf16[64,56,128]{2,1,0:T(8,128)(2,1)}), bf16[64,56,128]{2,1,0:T(8,128)(2,1)S(1)}, u32[]{:S(2)}, u32[]{:S(2)}) %all-to-all-start) | async-done | bytes 917536 | tf_op jit(solution)/shard_map/all_to_all | solution.py:367
  52.3 4.0 first_expert.1
  57.2 6.2 %all-to-all-start.1 = ((bf16[64,48,128]{2,1,0:T(8,128)(2,1)}), bf16[64,48,128]{2,1,0:T(8,128)(2,1)S(1)}, u32[]{:S(2)}, u32[]{:S(2)}) async-start(bf16[64,48,128]{2,1,0:T(8,128)(2,1)} %bitcast.123), calls=%async_computation.1 | async-start | bytes 1572864 | tf_op jit(solution)/shard_map/all_to_all | solution.py:367
  64.1 4.0 collective-permute-start
  68.1 4.0 collective-permute-start.2
  72.1 5.1 collective-permute-start.4
  77.2 4.8 collective-permute-start.3
  82.6 3.2 collective-permute-start.6
  87.1 3.1 collective-permute-start.7
  92.2 3.7 frame.9
  97.2 13.0 %collective-permute-done.3 = bf16[192,640]{1,0:T(8,128)(2,1)} collective-permute-done((bf16[192,640]{1,0:T(8,128)(2,1)}, bf16[192,640]{1,0:T(8,128)(2,1)}, u32[]{:S(2)}, u32[]{:S(2)}) %collective-permute-start.3) | collective-permute-done | bytes 245792 | tf_op jit(solution)/shard_map/ppermute | solution.py:393
  110.3 4.7 collective-permute-start.1
  115.8 3.1 frame.10.kept_ref
  121.2 13.3 %all-to-all-start.2 = ((bf16[64,24,128]{2,1,0:T(8,128)(2,1)}), bf16[64,24,128]{2,1,0:T(8,128)(2,1)}, u32[]{:S(2)}, u32[]{:S(2)}) async-start(bf16[64,24,128]{2,1,0:T(8,128)(2,1)} %bitcast.34), calls=%async_computation.2 | async-start | bytes 786432 | tf_op jit(solution)/shard_map/all_to_all | solution.py:367
  136.7 12.8 %all-to-all-done.2 = bf16[64,24,128]{2,1,0:T(8,128)(2,1)} async-done(((bf16[64,24,128]{2,1,0:T(8,128)(2,1)}), bf16[64,24,128]{2,1,0:T(8,128)(2,1)}, u32[]{:S(2)}, u32[]{:S(2)}) %all-to-all-start.2) | async-done | bytes 393248 | tf_op jit(solution)/shard_map/all_to_all | solution.py:367
  150.4 2.4 expert.7
  153.5 5.7 %all-to-all-start.3 = ((bf16[64,24,128]{2,1,0:T(8,128)(2,1)}), bf16[64,24,128]{2,1,0:T(8,128)(2,1)}, u32[]{:S(2)}, u32[]{:S(2)}) async-start(bf16[64,24,128]{2,1,0:T(8,128)(2,1)} %bitcast.111), calls=%async_computation.3 | async-start | bytes 786432 | tf_op jit(solution)/shard_map/all_to_all | solution.py:367
  163.8 10.6 %all-to-all-done.3 = bf16[64,24,128]{2,1,0:T(8,128)(2,1)} async-done(((bf16[64,24,128]{2,1,0:T(8,128)(2,1)}), bf16[64,24,128]{2,1,0:T(8,128)(2,1)}, u32[]{:S(2)}, u32[]{:S(2)}) %all-to-all-start.3) | async-done | bytes 393248 | tf_op jit(solution)/shard_map/all_to_all | solution.py:367
  177.8 3.6 frame.11.kept_ref
  187.7 5.8 %all-to-all-start.4 = ((bf16[64,24,128]{2,1,0:T(8,128)(2,1)}), bf16[64,24,128]{2,1,0:T(8,128)(2,1)}, u32[]{:S(2)}, u32[]{:S(2)}) async-start(bf16[64,24,128]{2,1,0:T(8,128)(2,1)} %bitcast.100), calls=%async_computation.4 | async-start | bytes 786432 | tf_op jit(solution)/shard_map/all_to_all | solution.py:367
  194.8 2.6 broadcast_select_fusion.refs_3_
  197.4 2.5 broadcast_select_fusion.2.refs_2_
  200.0 8.7 %all-to-all-done.4 = bf16[64,24,128]{2,1,0:T(8,128)(2,1)} async-done(((bf16[64,24,128]{2,1,0:T(8,128)(2,1)}), bf16[64,24,128]{2,1,0:T(8,128)(2,1)}, u32[]{:S(2)}, u32[]{:S(2)}) %all-to-all-start.4) | async-done | bytes 393248 | tf_op jit(solution)/shard_map/all_to_all | solution.py:367
  214.0 2.3 expert.8
  217.1 5.6 %all-to-all-start.5 = ((bf16[64,24,128]{2,1,0:T(8,128)(2,1)}), bf16[64,24,128]{2,1,0:T(8,128)(2,1)}, u32[]{:S(2)}, u32[]{:S(2)}) async-start(bf16[64,24,128]{2,1,0:T(8,128)(2,1)} %bitcast.112), calls=%async_computation.5 | async-start | bytes 786432 | tf_op jit(solution)/shard_map/all_to_all | solution.py:367
  226.2 11.6 %all-to-all-done.5 = bf16[64,24,128]{2,1,0:T(8,128)(2,1)} async-done(((bf16[64,24,128]{2,1,0:T(8,128)(2,1)}), bf16[64,24,128]{2,1,0:T(8,128)(2,1)}, u32[]{:S(2)}, u32[]{:S(2)}) %all-to-all-start.5) | async-done | bytes 393248 | tf_op jit(solution)/shard_map/all_to_all | solution.py:367
  241.2 4.3 frame.12.kept_ref
  248.9 20.4 %all_to_all.80 = bf16[64,24,128]{2,1,0:T(8,128)(2,1)S(1)} all-to-all(bf16[64,24,128]{2,1,0:T(8,128)(2,1)S(1)} %bitcast.101), channel_id=1, replica_groups=mesh['section'=8,'expert'=64] {'expert'}, dimensions={0} | all-to-all | bytes 786432 | tf_op jit(solution)/shard_map/all_to_all | solution.py:367
  271.5 20.4 %all_to_all.81 = bf16[64,24,128]{2,1,0:T(8,128)(2,1)S(1)} all-to-all(bf16[64,24,128]{2,1,0:T(8,128)(2,1)S(1)} %bitcast.118), channel_id=1, replica_groups=mesh['section'=8,'expert'=64] {'expert'}, dimensions={0} | all-to-all | bytes 786432 | tf_op jit(solution)/shard_map/all_to_all | solution.py:367
  291.9 4.3 frame.13.kept_ref
  299.6 20.4 %all_to_all.82 = bf16[64,24,128]{2,1,0:T(8,128)(2,1)S(1)} all-to-all(bf16[64,24,128]{2,1,0:T(8,128)(2,1)S(1)} %bitcast.102), channel_id=1, replica_groups=mesh['section'=8,'expert'=64] {'expert'}, dimensions={0} | all-to-all | bytes 786432 | tf_op jit(solution)/shard_map/all_to_all | solution.py:367
  323.7 20.4 %all_to_all.83 = bf16[64,24,128]{2,1,0:T(8,128)(2,1)S(1)} all-to-all(bf16[64,24,128]{2,1,0:T(8,128)(2,1)S(1)} %bitcast.120), channel_id=1, replica_groups=mesh['section'=8,'expert'=64] {'expert'}, dimensions={0} | all-to-all | bytes 786432 | tf_op jit(solution)/shard_map/all_to_all | solution.py:367
  344.1 4.4 frame.14.kept_ref
  351.9 20.4 %all_to_all.84 = bf16[64,24,128]{2,1,0:T(8,128)(2,1)S(1)} all-to-all(bf16[64,24,128]{2,1,0:T(8,128)(2,1)S(1)} %bitcast.103), channel_id=1, replica_groups=mesh['section'=8,'expert'=64] {'expert'}, dimensions={0} | all-to-all | bytes 786432 | tf_op jit(solution)/shard_map/all_to_all | solution.py:367
  373.7 20.4 %all_to_all.85 = bf16[64,24,128]{2,1,0:T(8,128)(2,1)S(1)} all-to-all(bf16[64,24,128]{2,1,0:T(8,128)(2,1)S(1)} %bitcast.122), channel_id=1, replica_groups=mesh['section'=8,'expert'=64] {'expert'}, dimensions={0} | all-to-all | bytes 786432 | tf_op jit(solution)/shard_map/all_to_all | solution.py:367
  394.1 4.4 frame.15.kept_ref
  401.8 20.4 %all_to_all.86 = bf16[64,24,128]{2,1,0:T(8,128)(2,1)S(1)} all-to-all(bf16[64,24,128]{2,1,0:T(8,128)(2,1)S(1)} %bitcast.104), channel_id=1, replica_groups=mesh['section'=8,'expert'=64] {'expert'}, dimensions={0} | all-to-all | bytes 786432 | tf_op jit(solution)/shard_map/all_to_all | solution.py:367
  425.9 20.4 %all_to_all.87 = bf16[64,24,128]{2,1,0:T(8,128)(2,1)S(1)} all-to-all(bf16[64,24,128]{2,1,0:T(8,128)(2,1)S(1)} %bitcast.115), channel_id=1, replica_groups=mesh['section'=8,'expert'=64] {'expert'}, dimensions={0} | all-to-all | bytes 786432 | tf_op jit(solution)/shard_map/all_to_all | solution.py:367
  446.3 4.3 frame.16.kept_ref
  452.0 29.3 %collective-permute-done.14.came_ref = bf16[128,8,128]{2,1,0:T(8,128)(2,1)} collective-permute-done((bf16[128,8,128]{2,1,0:T(8,128)(2,1)}, bf16[128,8,128]{2,1,0:T(8,128)(2,1)}, u32[]{:S(2)}, u32[]{:S(2)}) %collective-permute-start.14) | collective-permute-done | bytes 262176 | tf_op jit(solution)/shard_map/ppermute | solution.py:483
  482.6 20.5 %all_to_all.88 = bf16[64,24,128]{2,1,0:T(8,128)(2,1)S(1)} all-to-all(bf16[64,24,128]{2,1,0:T(8,128)(2,1)S(1)} %bitcast.105), channel_id=1, replica_groups=mesh['section'=8,'expert'=64] {'expert'}, dimensions={0} | all-to-all | bytes 786432 | tf_op jit(solution)/shard_map/all_to_all | solution.py:367
  505.2 5.4 %all-to-all-start.15 = ((bf16[64,24,128]{2,1,0:T(8,128)(2,1)}), bf16[64,24,128]{2,1,0:T(8,128)(2,1)S(1)}, u32[]{:S(2)}, u32[]{:S(2)}) async-start(bf16[64,24,128]{2,1,0:T(8,128)(2,1)} %bitcast.113), calls=%async_computation.15 | async-start | bytes 786432 | tf_op jit(solution)/shard_map/all_to_all | solution.py:367
  510.7 15.2 %all-to-all-done.15 = bf16[64,24,128]{2,1,0:T(8,128)(2,1)S(1)} async-done(((bf16[64,24,128]{2,1,0:T(8,128)(2,1)}), bf16[64,24,128]{2,1,0:T(8,128)(2,1)S(1)}, u32[]{:S(2)}, u32[]{:S(2)}) %all-to-all-start.15) | async-done | bytes 393248 | tf_op jit(solution)/shard_map/all_to_all | solution.py:367
  526.8 3.6 frame.17
  531.9 8.2 %collective-permute-done.15 = bf16[128,8,128]{2,1,0:T(8,128)(2,1)S(1)} collective-permute-done((bf16[128,8,128]{2,1,0:T(8,128)(2,1)S(1)}, bf16[128,8,128]{2,1,0:T(8,128)(2,1)S(1)}, u32[]{:S(2)}, u32[]{:S(2)}) %collective-permute-start.15) | collective-permute-done | bytes 262176 | tf_op jit(solution)/shard_map/ppermute | solution.py:486
  (258 shorter events, 78.2 us)
Async XLA Ops:
  0.0 26.7 %copy-start.6 = (bf16[1,1,1024,640]{3,2,1,0:T(8,128)(2,1)S(1)}, bf16[1,1,1024,640]{3,2,1,0:T(8,128)(2,1)}, u32[]{:S(2)}) copy-start(bf16[1,1,1024,640]{3,2,1,0:T(8,128)(2,1)} %param.20) | copy-start | bytes 3932164
  15.1 37.2 %all-to-all-start = ((bf16[64,56,128]{2,1,0:T(8,128)(2,1)}), bf16[64,56,128]{2,1,0:T(8,128)(2,1)S(1)}, u32[]{:S(2)}, u32[]{:S(2)}) async-start(bf16[64,56,128]{2,1,0:T(8,128)(2,1)} %bitcast.124), calls=%async_computation | async-start | bytes 1835008 | tf_op jit(solution)/shard_map/all_to_all | solution.py:367
  26.7 64.2 %collective-permute-start.5 = (bf16[1024,640]{1,0:T(8,128)(2,1)S(1)}, bf16[1024,640]{1,0:T(8,128)(2,1)}, u32[]{:S(2)}, u32[]{:S(2)}) collective-permute-start(bf16[1024,640]{1,0:T(8,128)(2,1)S(1)} %bitcast.94), channel_id=1, source_target_pairs={{0,64},{64,128},{128,192},{192,256},{256,320},{320,384},{384,448},... | collective-permute-start | bytes 3932168 | tf_op jit(solution)/shard_map/ppermute | solution.py:393
  33.2 23.0 %copy-start.27 = (bf16[192,640]{1,0:T(8,128)(2,1)}, bf16[192,640]{1,0:T(8,128)(2,1)S(1)}, u32[]{:S(2)}) copy-start(bf16[192,640]{1,0:T(8,128)(2,1)S(1)} %get-tuple-element.79.refs_2_) | copy-start | bytes 737284
  33.2 24.0 %copy-start.62 = (bf16[192,640]{1,0:T(8,128)(2,1)}, bf16[192,640]{1,0:T(8,128)(2,1)S(1)}, u32[]{:S(2)}) copy-start(bf16[192,640]{1,0:T(8,128)(2,1)S(1)} %get-tuple-element.97.refs_3_) | copy-start | bytes 737284
  57.2 33.7 %copy-start.69 = (bf16[192,128]{1,0:T(8,128)(2,1)}, bf16[192,128]{1,0:T(8,128)(2,1)S(1)}, u32[]{:S(2)}) copy-start(bf16[192,128]{1,0:T(8,128)(2,1)S(1)} %get-tuple-element.75) | copy-start | bytes 147460
  57.2 24.8 %copy-start.92 = (s32[2,1]{0,1:T(1,128)S(1)}, s32[2,1]{0,1:T(1,128)}, u32[]{:S(2)}) copy-start(s32[2,1]{0,1:T(1,128)} %param.13) | copy-start | bytes 28
  57.2 33.0 %copy-start.30 = (bf16[192,640]{1,0:T(8,128)(2,1)S(1)}, bf16[192,640]{1,0:T(8,128)(2,1)}, u32[]{:S(2)}) copy-start(bf16[192,640]{1,0:T(8,128)(2,1)} %copy-done.29) | copy-start | bytes 737284
  57.2 33.9 %all-to-all-start.1 = ((bf16[64,48,128]{2,1,0:T(8,128)(2,1)}), bf16[64,48,128]{2,1,0:T(8,128)(2,1)S(1)}, u32[]{:S(2)}, u32[]{:S(2)}) async-start(bf16[64,48,128]{2,1,0:T(8,128)(2,1)} %bitcast.123), calls=%async_computation.1 | async-start | bytes 1572864 | tf_op jit(solution)/shard_map/all_to_all | solution.py:367
  64.1 18.6 %collective-permute-start = (bf16[273,128]{1,0:T(8,128)(2,1)S(1)}, bf16[273,128]{1,0:T(8,128)(2,1)S(1)}, u32[]{:S(2)}, u32[]{:S(2)}) collective-permute-start(bf16[273,128]{1,0:T(8,128)(2,1)S(1)} %pad_maximum_fusion.1), channel_id=1, source_target_pairs={{0,64},{64,128},{128,192},{192,256},{256,320},{320,384},{384,448},... | collective-permute-start | bytes 209672 | tf_op jit(solution)/shard_map/ppermute | solution.py:393
  68.1 19.0 %collective-permute-start.2 = (bf16[192,640]{1,0:T(8,128)(2,1)S(1)}, bf16[192,640]{1,0:T(8,128)(2,1)S(1)}, u32[]{:S(2)}, u32[]{:S(2)}) collective-permute-start(bf16[192,640]{1,0:T(8,128)(2,1)S(1)} %copy-done.64), channel_id=1, source_target_pairs={{0,64},{64,128},{128,192},{192,256},{256,320},{320,384},{384,448},... | collective-permute-start | bytes 737288 | tf_op jit(solution)/shard_map/ppermute | solution.py:393
  72.1 62.4 %collective-permute-start.4 = (bf16[640,1024]{1,0:T(8,128)(2,1)}, bf16[640,1024]{1,0:T(8,128)(2,1)}, u32[]{:S(2)}, u32[]{:S(2)}) collective-permute-start(bf16[640,1024]{1,0:T(8,128)(2,1)} %bitcast.15.refs_4_), channel_id=1, source_target_pairs={{0,64},{64,128},{128,192},{192,256},{256,320},{320,384},{384,448},... | collective-permute-start | bytes 3932168 | tf_op jit(solution)/shard_map/ppermute | solution.py:393
  77.2 33.1 %collective-permute-start.3 = (bf16[192,640]{1,0:T(8,128)(2,1)}, bf16[192,640]{1,0:T(8,128)(2,1)}, u32[]{:S(2)}, u32[]{:S(2)}) collective-permute-start(bf16[192,640]{1,0:T(8,128)(2,1)} %copy-done.62), channel_id=1, source_target_pairs={{0,64},{64,128},{128,192},{192,256},{256,320},{320,384},{384,448},... | collective-permute-start | bytes 737288 | tf_op jit(solution)/shard_map/ppermute | solution.py:393
  82.6 79.4 %collective-permute-start.6 = (bf16[128,8,128]{2,1,0:T(8,128)(2,1)}, bf16[128,8,128]{2,1,0:T(8,128)(2,1)}, u32[]{:S(2)}, u32[]{:S(2)}) collective-permute-start(bf16[128,8,128]{2,1,0:T(8,128)(2,1)} %get-tuple-element.53.normed_ref), channel_id=1, source_target_pairs={{0,64},{64,128},{128,192},{192,256},{256,320},{320,384},{384,448},... | collective-permute-start | bytes 786440 | tf_op jit(solution)/shard_map/ppermute | solution.py:393
  87.1 75.0 %collective-permute-start.7 = (bf16[128,8,128]{2,1,0:T(8,128)(2,1)}, bf16[128,8,128]{2,1,0:T(8,128)(2,1)}, u32[]{:S(2)}, u32[]{:S(2)}) collective-permute-start(bf16[128,8,128]{2,1,0:T(8,128)(2,1)} %get-tuple-element.54.slope_ref), channel_id=1, source_target_pairs={{0,64},{64,128},{128,192},{192,256},{256,320},{320,384},{384,448},... | collective-permute-start | bytes 786440 | tf_op jit(solution)/shard_map/ppermute | solution.py:393
  91.1 23.9 %copy-start.28 = (bf16[192,640]{1,0:T(8,128)(2,1)S(1)}, bf16[192,640]{1,0:T(8,128)(2,1)}, u32[]{:S(2)}) copy-start(bf16[192,640]{1,0:T(8,128)(2,1)} %copy-done.27) | copy-start | bytes 737284
  92.1 23.6 %copy-start.42 = (bf16[128,8,128]{2,1,0:T(8,128)(2,1)S(1)}, bf16[128,8,128]{2,1,0:T(8,128)(2,1)}, u32[]{:S(2)}) copy-start(bf16[128,8,128]{2,1,0:T(8,128)(2,1)} %get-tuple-element.89.normed_ref) | copy-start | bytes 786436
  92.1 23.6 %copy-start.44 = (bf16[128,8,128]{2,1,0:T(8,128)(2,1)S(1)}, bf16[128,8,128]{2,1,0:T(8,128)(2,1)}, u32[]{:S(2)}) copy-start(bf16[128,8,128]{2,1,0:T(8,128)(2,1)} %get-tuple-element.91.slope_ref) | copy-start | bytes 786436
  92.1 23.6 %copy-start.56 = (bf16[128,8,128]{2,1,0:T(8,128)(2,1)S(1)}, bf16[128,8,128]{2,1,0:T(8,128)(2,1)}, u32[]{:S(2)}) copy-start(bf16[128,8,128]{2,1,0:T(8,128)(2,1)} %get-tuple-element.71.kept_ref.came_ref) | copy-start | bytes 786436
  92.1 23.6 %copy-start.86 = (s32[128]{0:T(128)S(1)}, s32[128]{0:T(128)}, u32[]{:S(2)}) copy-start(s32[128]{0:T(128)} %get-tuple-element.111.row_ref) | copy-start | bytes 1540
  95.8 23.0 %copy-start.40 = (bf16[128,8,128]{2,1,0:T(8,128)(2,1)}, bf16[128,8,128]{2,1,0:T(8,128)(2,1)S(1)}, u32[]{:S(2)}) copy-start(bf16[128,8,128]{2,1,0:T(8,128)(2,1)S(1)} %frame.9) | copy-start | bytes 786436
  95.9 23.0 %collective-permute-start.8 = (bf16[128,8,128]{2,1,0:T(8,128)(2,1)S(1)}, bf16[128,8,128]{2,1,0:T(8,128)(2,1)S(1)}, u32[]{:S(2)}, u32[]{:S(2)}) collective-permute-start(bf16[128,8,128]{2,1,0:T(8,128)(2,1)S(1)} %frame.9), channel_id=1, source_target_pairs={{448,384},{449,385},{450,386},{451,387},{452,388},{453,389},{454,3... | collective-permute-start | bytes 786440 | tf_op jit(solution)/shard_map/ppermute | solution.py:445
  110.3 25.8 %collective-permute-start.1 = (bf16[192,128]{1,0:T(8,128)(2,1)}, bf16[192,128]{1,0:T(8,128)(2,1)}, u32[]{:S(2)}, u32[]{:S(2)}) collective-permute-start(bf16[192,128]{1,0:T(8,128)(2,1)} %get-tuple-element.70), channel_id=1, source_target_pairs={{0,64},{64,128},{128,192},{192,256},{256,320},{320,384},{384,448},... | collective-permute-start | bytes 147464 | tf_op jit(solution)/shard_map/ppermute | solution.py:393
  121.2 28.4 %all-to-all-start.2 = ((bf16[64,24,128]{2,1,0:T(8,128)(2,1)}), bf16[64,24,128]{2,1,0:T(8,128)(2,1)}, u32[]{:S(2)}, u32[]{:S(2)}) async-start(bf16[64,24,128]{2,1,0:T(8,128)(2,1)} %bitcast.34), calls=%async_computation.2 | async-start | bytes 786432 | tf_op jit(solution)/shard_map/all_to_all | solution.py:367
  153.5 20.9 %all-to-all-start.3 = ((bf16[64,24,128]{2,1,0:T(8,128)(2,1)}), bf16[64,24,128]{2,1,0:T(8,128)(2,1)}, u32[]{:S(2)}, u32[]{:S(2)}) async-start(bf16[64,24,128]{2,1,0:T(8,128)(2,1)} %bitcast.111), calls=%async_computation.3 | async-start | bytes 786432 | tf_op jit(solution)/shard_map/all_to_all | solution.py:367
  181.4 4.8 collective-permute-start.9
  187.7 20.9 %all-to-all-start.4 = ((bf16[64,24,128]{2,1,0:T(8,128)(2,1)}), bf16[64,24,128]{2,1,0:T(8,128)(2,1)}, u32[]{:S(2)}, u32[]{:S(2)}) async-start(bf16[64,24,128]{2,1,0:T(8,128)(2,1)} %bitcast.100), calls=%async_computation.4 | async-start | bytes 786432 | tf_op jit(solution)/shard_map/all_to_all | solution.py:367
  217.1 20.7 %all-to-all-start.5 = ((bf16[64,24,128]{2,1,0:T(8,128)(2,1)}), bf16[64,24,128]{2,1,0:T(8,128)(2,1)}, u32[]{:S(2)}, u32[]{:S(2)}) async-start(bf16[64,24,128]{2,1,0:T(8,128)(2,1)} %bitcast.112), calls=%async_computation.5 | async-start | bytes 786432 | tf_op jit(solution)/shard_map/all_to_all | solution.py:367
  245.5 1.4 collective-permute-start.10
  296.2 1.4 collective-permute-start.11
  297.6 22.4 %copy-start.1 = (bf16[1024,640]{1,0:T(8,128)(2,1)S(1)}, bf16[1024,640]{1,0:T(8,128)(2,1)}, u32[]{:S(2)}) copy-start(bf16[1024,640]{1,0:T(8,128)(2,1)} %broadcast_select_fusion.refs_3_) | copy-start | bytes 3932164
  297.6 22.4 %copy-start.32 = (bf16[192,640]{1,0:T(8,128)(2,1)S(1)}, bf16[192,640]{1,0:T(8,128)(2,1)}, u32[]{:S(2)}) copy-start(bf16[192,640]{1,0:T(8,128)(2,1)} %get-tuple-element.119.refs_1_) | copy-start | bytes 737284
  297.6 22.4 %copy-start.66 = (bf16[192,128]{1,0:T(8,128)(2,1)S(1)}, bf16[192,128]{1,0:T(8,128)(2,1)}, u32[]{:S(2)}) copy-start(bf16[192,128]{1,0:T(8,128)(2,1)} %broadcast_select_fusion.17.gate_ref) | copy-start | bytes 147460
  348.5 1.4 collective-permute-start.12
  349.8 22.4 %copy-start.15 = (bf16[192,640]{1,0:T(8,128)(2,1)S(1)}, bf16[192,640]{1,0:T(8,128)(2,1)}, u32[]{:S(2)}) copy-start(bf16[192,640]{1,0:T(8,128)(2,1)} %broadcast_select_fusion.14.refs_0_) | copy-start | bytes 737284
  349.9 22.4 %copy-start.19 = (bf16[192,640]{1,0:T(8,128)(2,1)S(1)}, bf16[192,640]{1,0:T(8,128)(2,1)}, u32[]{:S(2)}) copy-start(bf16[192,640]{1,0:T(8,128)(2,1)} %broadcast_select_fusion.13.refs_1_) | copy-start | bytes 737284
  349.9 22.4 %copy-start.54 = (bf16[192,128]{1,0:T(8,128)(2,1)S(1)}, bf16[192,128]{1,0:T(8,128)(2,1)}, u32[]{:S(2)}) copy-start(bf16[192,128]{1,0:T(8,128)(2,1)} %broadcast_select_fusion.18.gate_ref) | copy-start | bytes 147460
  398.4 1.4 collective-permute-start.13
  399.8 22.4 %copy-start.2 = (bf16[1024,640]{1,0:T(8,128)(2,1)S(1)}, bf16[1024,640]{1,0:T(8,128)(2,1)}, u32[]{:S(2)}) copy-start(bf16[1024,640]{1,0:T(8,128)(2,1)} %broadcast_select_fusion.refs_3_) | copy-start | bytes 3932164
  399.8 22.4 %copy-start.33 = (bf16[192,640]{1,0:T(8,128)(2,1)S(1)}, bf16[192,640]{1,0:T(8,128)(2,1)}, u32[]{:S(2)}) copy-start(bf16[192,640]{1,0:T(8,128)(2,1)} %get-tuple-element.119.refs_1_) | copy-start | bytes 737284
  399.8 22.4 %copy-start.67 = (bf16[192,128]{1,0:T(8,128)(2,1)S(1)}, bf16[192,128]{1,0:T(8,128)(2,1)}, u32[]{:S(2)}) copy-start(bf16[192,128]{1,0:T(8,128)(2,1)} %broadcast_select_fusion.17.gate_ref) | copy-start | bytes 147460
  425.9 55.4 %copy-start.79 = (s32[128]{0:T(128)S(1)}, s32[128]{0:T(128)}, u32[]{:S(2)}) copy-start(s32[128]{0:T(128)} %copy-done.73) | copy-start | bytes 1540
  450.7 30.6 %collective-permute-start.14 = (bf16[128,8,128]{2,1,0:T(8,128)(2,1)}, bf16[128,8,128]{2,1,0:T(8,128)(2,1)}, u32[]{:S(2)}, u32[]{:S(2)}) collective-permute-start(bf16[128,8,128]{2,1,0:T(8,128)(2,1)} %frame.16.kept_ref), channel_id=1, source_target_pairs={{128,0},{129,1},{130,2},{131,3},{132,4},{133,5},{134,6},{135,7},{1... | collective-permute-start | bytes 786440 | tf_op jit(solution)/shard_map/ppermute | solution.py:483
  452.0 51.1 %copy-start.16 = (bf16[192,640]{1,0:T(8,128)(2,1)S(1)}, bf16[192,640]{1,0:T(8,128)(2,1)}, u32[]{:S(2)}) copy-start(bf16[192,640]{1,0:T(8,128)(2,1)} %broadcast_select_fusion.14.refs_0_) | copy-start | bytes 737284
  452.0 51.1 %copy-start.20 = (bf16[192,640]{1,0:T(8,128)(2,1)S(1)}, bf16[192,640]{1,0:T(8,128)(2,1)}, u32[]{:S(2)}) copy-start(bf16[192,640]{1,0:T(8,128)(2,1)} %broadcast_select_fusion.13.refs_1_) | copy-start | bytes 737284
  452.0 51.1 %copy-start.55 = (bf16[192,128]{1,0:T(8,128)(2,1)S(1)}, bf16[192,128]{1,0:T(8,128)(2,1)}, u32[]{:S(2)}) copy-start(bf16[192,128]{1,0:T(8,128)(2,1)} %broadcast_select_fusion.18.gate_ref) | copy-start | bytes 147460
  505.2 20.6 %all-to-all-start.15 = ((bf16[64,24,128]{2,1,0:T(8,128)(2,1)}), bf16[64,24,128]{2,1,0:T(8,128)(2,1)S(1)}, u32[]{:S(2)}, u32[]{:S(2)}) async-start(bf16[64,24,128]{2,1,0:T(8,128)(2,1)} %bitcast.113), calls=%async_computation.15 | async-start | bytes 786432 | tf_op jit(solution)/shard_map/all_to_all | solution.py:367
  530.6 9.5 %collective-permute-start.15 = (bf16[128,8,128]{2,1,0:T(8,128)(2,1)S(1)}, bf16[128,8,128]{2,1,0:T(8,128)(2,1)S(1)}, u32[]{:S(2)}, u32[]{:S(2)}) collective-permute-start(bf16[128,8,128]{2,1,0:T(8,128)(2,1)S(1)} %select_select_fusion.1), channel_id=1, source_target_pairs={{64,0},{128,64},{192,128},{256,192},{320,256},{384,320},{448,384},... | collective-permute-start | bytes 786440 | tf_op jit(solution)/shard_map/ppermute | solution.py:486
  (70 other events, 598.6 us)
